TPU v7x, 128 devices: a whole 4x4x4 slice. The times are simulated.
128 devices in a mesh: section: 4 (over z), dp: 32 (over x, y, core).
Axes of the slice: x: 4, y: 4, z: 4, core: 2. Of those that a mesh axis runs over, the one named last changes fastest.
Arguments:
- gradient: float32 [4, 32, 256, 4096], P('section', 'dp'), may hold values from -6 to 6
- dither: int32 [4, 32, 256, 4096], P('section', 'dp'), may hold values from 0 to 255
- sign_bits: int32 [4096], replicated, may hold values from 0 to 1
- levels: float32 [16], replicated, may hold values from -1 to 1, as said below
- layout: int32 [256], replicated, may hold values from 0 to 255, each once
- master: float32 [4, 256, 4096], P('section', 'dp'), may hold values from -6 to 6
- first_moment: float32 [4, 256, 4096], P('section', 'dp'), may hold values from -4 to 4
- second_moment: float32 [4, 256, 4096], P('section', 'dp'), may hold values from 0.05 to 2
Outputs:
- updated_master: float32 [4, 256, 4096], P('section', 'dp')
- updated_first: float32 [4, 256, 4096], P('section', 'dp')
- updated_second: float32 [4, 256, 4096], P('section', 'dp')
- parameters: bfloat16 [4, 256, 4096], P('section')
Inputs may be any that keep to these rules, and one draw needn't show every extreme that they name: `levels`: strictly increasing; the first is -1 and the last 1; neighbouring levels differ by at least 1/30. `layout`: each block number once.
All inputs are finite; a program needn't handle non-finite values.
Results may differ from a plain program's by a relative error of at most 0.001.
The roundings to bfloat16 on the way count: a program that leaves them out, or rounds other values in their place, can miss the bound.
Values may be sent and summed in bfloat16 or wider, within the bound.
No kernel may reach another device: no remote copies, remote signals or barrier semaphores. Data moves between devices by JAX's collectives and lax.ppermute only.
A program may use at most 64 MiB of HBM per device.

v0:
```python
import math

import jax
import jax.numpy as jnp
from jax import lax
from jax.sharding import PartitionSpec as P

adam_epsilon = 1e-08
learning_rate = 0.02
weight_decay = 0.1
first_decay = 0.9
second_decay = 0.95
dither_steps = 256.0


def from_everyone(shard, axis):
    copies = jnp.broadcast_to(shard, (lax.axis_size(axis), *shard.shape))
    return lax.all_to_all(copies, axis, split_axis=0, concat_axis=0, tiled=True)


def over_copies(shard, axis):
    everything = from_everyone(shard, axis)
    return jnp.max(everything, axis=0)


def laid_out(pieces, dim):
    pieces = jnp.moveaxis(pieces, 0, dim)
    shape = pieces.shape
    return pieces.reshape(*shape[:dim], shape[dim] * shape[dim + 1], *shape[dim + 2 :])


def gathered_copies(shard, axis, dim):
    pieces = from_everyone(shard, axis)
    return laid_out(pieces, dim)


def hadamard_table(edge_length):
    row_numbers = lax.broadcasted_iota(jnp.int32, (edge_length, edge_length), 0)
    column_numbers = lax.broadcasted_iota(jnp.int32, (edge_length, edge_length), 1)
    common = jnp.bitwise_and(row_numbers, column_numbers)
    parity = jnp.zeros((edge_length, edge_length), jnp.int32)
    for bit_number in range(edge_length.bit_length() - 1):
        parity = parity + jnp.bitwise_and(jnp.right_shift(common, bit_number), 1)
    parity = parity % 2
    return (1 - 2 * parity).astype(jnp.float32)


def square_transform(blocks):
    edge_length = math.isqrt(blocks.shape[-1])
    table = hadamard_table(edge_length)
    folded = blocks.reshape(-1, edge_length, edge_length)
    turned = jnp.einsum("ac,ncd,db->nab", table, folded, table, precision=lax.Precision.HIGHEST)
    return turned.reshape(blocks.shape) / edge_length


def rotate(blocks, flips):
    return square_transform(blocks * flips)


def unrotate(blocks, flips):
    return square_transform(blocks) * flips


def encode(ratios, levels):
    relaxed = jnp.zeros_like(ratios)
    for position in range(levels.shape[0] - 1):
        spacing = levels[position + 1] - levels[position]
        relaxed = relaxed + jnp.clip((ratios - levels[position]) / spacing, 0.0, 1.0)
    return relaxed


def decode(symbols, levels):
    values = jnp.zeros_like(symbols) + levels[0]
    for position in range(levels.shape[0] - 1):
        spacing = levels[position + 1] - levels[position]
        values = values + spacing * jnp.clip(symbols - position, 0.0, 1.0)
    return values


def local(gradient, dither, sign_bits, levels, layout, master, first_moment, second_moment):
    flips = (1 - 2 * sign_bits).astype(jnp.float32)
    rotated = rotate(gradient[0, 0], flips)
    peaks = jnp.max(jnp.abs(rotated), axis=1)
    block_scale = over_copies(peaks, "dp") + 1e-06
    offsets = (dither[0, 0].astype(jnp.float32) + 0.5) / dither_steps - 0.5
    symbols = (encode(rotated / block_scale[:, None], levels) + offsets).astype(jnp.bfloat16)
    slotted = jnp.take(symbols, layout, axis=0)
    groups = lax.axis_size("dp")
    block_count = slotted.shape[0]
    owned = block_count // groups
    first_slot = lax.axis_index("dp") * owned
    slot_scale = lax.dynamic_slice_in_dim(jnp.take(block_scale, layout), first_slot, owned)
    summed_codes = jnp.sum(
        decode(
            lax.all_to_all(
                slotted.reshape(groups, owned, slotted.shape[1]),
                "dp",
                split_axis=0,
                concat_axis=0,
                tiled=True,
            ).astype(jnp.float32),
            levels,
        ),
        axis=0,
    )
    grads = unrotate(summed_codes * slot_scale[:, None], flips)
    updated_first = first_decay * first_moment[0] + (1.0 - first_decay) * grads
    updated_second = second_decay * second_moment[0] + (1.0 - second_decay) * grads * grads
    updated_master = master[0] - learning_rate * (
        updated_first / (jnp.sqrt(updated_second) + adam_epsilon) + weight_decay * master[0]
    )
    gathered = gathered_copies(updated_master.astype(jnp.bfloat16), "dp", 0)
    inverse = jnp.argsort(layout)
    parameters = jnp.take(gathered, inverse, axis=0)
    return (updated_master[None], updated_first[None], updated_second[None], parameters[None])


def solution(mesh):
    placed = (
        P("section", "dp", None, None),
        P("section", "dp", None, None),
        P(),
        P(),
        P(),
        P("section", "dp", None),
        P("section", "dp", None),
        P("section", "dp", None),
    )
    return jax.shard_map(
        local,
        mesh=mesh,
        in_specs=placed,
        out_specs=(
            P("section", "dp", None),
            P("section", "dp", None),
            P("section", "dp", None),
            P("section", None, None),
        ),
        check_vma=False,
    )
```

profile of v0, /device:TPU:1, one launch (start us, length us, event | category | flops | bytes accessed | tf_op | source)
XLA Modules:
  0.0 172.3 jit_solution(17070775594421589876)
XLA Ops:
  0.6 0.0 copy-start.4
  0.6 5.6 %copy.30 = f32[1,1,256,4096]{2,3,1,0:T(8,128)} copy(f32[1,1,256,4096]{3,2,1,0:T(8,128)} %param.10) | data formatting | bytes 8388608 | tf_op args[0]
  6.2 0.0 copy-done.4
  6.3 0.1 mul.245
  6.3 2.6 %broadcast_multiply_fusion = f32[256,64,64]{0,2,1:T(8,128)S(1)} fusion(f32[256,64,64]{0,2,1:T(8,128)} %bitcast.56, f32[64,64]{1,0:T(8,128)S(1)} %mul.245), kind=kLoop, calls=%fused_computation.73 | loop fusion | flops 1048576 | bytes 8404992 | tf_op jit(solution)/shard_map/mul | solution.py:57
  8.9 6.6 %fusion.47 = f32[256,64,64]{0,2,1:T(8,128)S(1)} fusion(f32[256,64,64]{0,2,1:T(8,128)S(1)} %broadcast_multiply_fusion), kind=kOutput, calls=%fused_computation.66 | convolution fusion | flops 805437440 | bytes 8388608 | tf_op jit(solution)/shard_map/ac,ncd,db->nab/dot_general | solution.py:52
  15.6 0.0 copy-start.3
  15.6 0.0 copy-start.5
  15.6 7.0 %abs_reduce_fusion = (f32[256]{0:T(256)S(1)}, f32[256,64,64]{0,2,1:T(8,128)}) fusion(f32[256,64,64]{0,2,1:T(8,128)S(1)} %fusion.47), kind=kOutput, calls=%fused_computation.68 | convolution fusion | flops 808582912 | bytes 8389632 | tf_op jit(solution)/shard_map/ac,ncd,db->nab/dot_general | solution.py:52
  22.6 0.6 broadcast_in_dim.33
  23.2 8.6 %all-to-all-start = ((f32[32,1,256]{2,1,0:T(1,128)}), f32[32,1,256]{2,1,0:T(1,128)S(1)}, u32[]{:S(2)}, u32[]{:S(2)}) async-start(f32[32,1,256]{2,1,0:T(1,128)} %broadcast_in_dim.33), calls=%async_computation | async-start | bytes 65536 | tf_op jit(solution)/shard_map/all_to_all | solution.py:18
  31.8 0.0 copy-done.3
  31.9 0.7 fusion.124
  32.6 0.0 copy-done.5
  32.6 5.7 %copy.35 = f32[256,4096]{1,0:T(8,128)} copy(f32[256,4096]{0,1:T(8,128)} %bitcast.55) | data formatting | bytes 8388608 | tf_op jit(solution)/shard_map/div | solution.py:53
  56.9 0.0 all-to-all-done
  56.9 0.1 reduce_max.19
  57.0 1.9 %gather_fusion = f32[256]{0:T(256)S(1)} fusion(f32[256]{0:T(256)S(1)} %broadcast_add_fusion, s32[1024]{0:T(1024)S(1)} %pad_clamp_fusion.1), kind=kCustom, calls=%fused_computation.2 | custom fusion | bytes 3072 | tf_op jit(solution)/shard_map/jit(_take)/gather | solution.py:92
  59.0 20.1 %fusion.44 = bf16[256,4096]{1,0:T(8,128)(2,1)S(1)} fusion(s32[1,1,256,4096]{3,2,1,0:T(8,128)} %param.11, f32[256,4096]{1,0:T(8,128)} %copy.35, f32[]{:T(128)S(6)} %sub.280, f32[]{:T(128)} %bitcast.18, f32[]{:T(128)S(6)} %sub.277, f32[]{:T(128)} %bitcast.17, f32[]{:T(128)S(6)} %sub.274, f32[]{:T(128)} %bitcast.16, f32[]{:T(128)S(6)} %sub.271, f32[]{:T(128)} %bitcast.15, ...), kind=kLoop, calls=%fused_computation.63 | loop fusion | flops 69206016 | bytes 10486904 | tf_op jit(solution)/shard_map/convert_element_type | solution.py:86
  79.1 3.2 %gather_fusion.1 = bf16[256,4096]{1,0:T(8,128)(2,1)} fusion(bf16[256,4096]{1,0:T(8,128)(2,1)S(1)} %fusion.44, s32[1024]{0:T(1024)S(1)} %pad_clamp_fusion.1), kind=kCustom, calls=%fused_computation.clone | custom fusion | bytes 4195328 | tf_op jit(solution)/shard_map/jit(_take)/gather | solution.py:87
  82.3 3.2 %select_bitcast_fusion.1 = bf16[32,8,4096]{2,1,0:T(8,128)(2,1)} fusion(bf16[256,4096]{1,0:T(8,128)(2,1)} %gather_fusion.1, pred[256]{0:T(512)(128)(4,1)S(1)} %get-tuple-element.11), kind=kLoop, calls=%fused_computation.72 | loop fusion | flops 1048576 | bytes 4194560 | tf_op jit(solution)/shard_map/reshape | solution.py:96
  85.5 0.0 copy-start
  85.5 0.0 copy-start.1
  85.5 0.0 copy-start.2
  85.5 7.5 %all-to-all-start.1 = ((bf16[32,8,4096]{2,1,0:T(8,128)(2,1)}), bf16[32,8,4096]{2,1,0:T(8,128)(2,1)S(1)}, u32[]{:S(2)}, u32[]{:S(2)}) async-start(bf16[32,8,4096]{2,1,0:T(8,128)(2,1)} %select_bitcast_fusion.1), calls=%async_computation.1 | async-start | bytes 4194304 | tf_op jit(solution)/shard_map/all_to_all | solution.py:95
  93.0 0.1 dynamic_slice.3
  93.1 28.2 %all-to-all-done.1 = bf16[32,8,4096]{2,1,0:T(8,128)(2,1)S(1)} async-done(((bf16[32,8,4096]{2,1,0:T(8,128)(2,1)}), bf16[32,8,4096]{2,1,0:T(8,128)(2,1)S(1)}, u32[]{:S(2)}, u32[]{:S(2)}) %all-to-all-start.1) | async-done | bytes 2097184 | tf_op jit(solution)/shard_map/all_to_all | solution.py:95
  121.3 8.9 %fusion.49 = f32[8,4096]{1,0:T(8,128)S(1)} fusion(bf16[32,8,4096]{2,1,0:T(8,128)(2,1)S(1)} %all-to-all-done.1, f32[]{:T(128)S(6)} %sub.280, f32[]{:T(128)S(6)} %sub.277, f32[]{:T(128)S(6)} %sub.274, f32[]{:T(128)S(6)} %sub.271, f32[]{:T(128)S(6)} %sub.268, f32[]{:T(128)S(6)} %sub.265, f32[]{:T(128)S(6)} %sub.262, f32[]{:T(128)S(6)} %sub.259, f32[]{:T(128)S(6)} %sub.256, ...), kind=kLoop, calls=%fused_computation.69 | loop fusion | flops 63930368 | bytes 2228288 | tf_op jit(solution)/shard_map/reduce_sum | solution.py:93
  130.3 0.1 reduce_sum.12
  130.4 0.5 fusion.53
  130.8 0.4 fusion.71
  131.2 0.1 reshape.137
  131.3 0.0 copy-done
  131.4 0.0 copy-done.1
  131.4 0.0 copy-done.2
  131.4 0.1 fusion.64
  131.5 1.6 broadcast_in_dim.36
  133.1 4.5 %all-to-all-start.2 = ((bf16[32,8,4096]{2,1,0:T(8,128)(2,1)}), bf16[32,8,4096]{2,1,0:T(8,128)(2,1)S(1)}, u32[]{:S(2)}, u32[]{:S(2)}) async-start(bf16[32,8,4096]{2,1,0:T(8,128)(2,1)} %broadcast_in_dim.36), calls=%async_computation.2 | async-start | bytes 4194304 | tf_op jit(solution)/shard_map/all_to_all | solution.py:18
  137.6 3.2 %sort.17 = (s32[256]{0:T(256)}, s32[256]{0:T(256)S(1)}) sort(s32[256]{0:T(256)S(1)} %copy-done.5, s32[256]{0:T(256)S(1)} %iota.32), dimensions={0}, to_apply=%region_3.5 | sort | flops 2048 | bytes 4096 | tf_op jit(solution)/shard_map/jit(argsort)/sort | solution.py:113
  140.8 0.1 reshape.136
  140.9 0.8 multiply_subtract_fusion
  141.7 24.3 %all-to-all-done.2 = bf16[32,8,4096]{2,1,0:T(8,128)(2,1)S(1)} async-done(((bf16[32,8,4096]{2,1,0:T(8,128)(2,1)}), bf16[32,8,4096]{2,1,0:T(8,128)(2,1)S(1)}, u32[]{:S(2)}, u32[]{:S(2)}) %all-to-all-start.2) | async-done | bytes 2097184 | tf_op jit(solution)/shard_map/all_to_all | solution.py:18
  166.0 3.2 %gather_fusion.2 = bf16[256,4096]{1,0:T(8,128)(2,1)} fusion(bf16[256,4096]{1,0:T(8,128)(2,1)S(1)} %bitcast.54, s32[1024]{0:T(1024)S(1)} %pad_clamp_fusion), kind=kCustom, calls=%fused_computation.1.clone | custom fusion | bytes 4195328 | tf_op jit(solution)/shard_map/jit(_take)/gather | solution.py:114
  169.1 3.2 %select_bitcast_fusion = bf16[1,256,4096]{2,1,0:T(8,128)(2,1)} fusion(bf16[256,4096]{1,0:T(8,128)(2,1)} %gather_fusion.2, pred[256]{0:T(512)(128)(4,1)S(1)} %compare_and_fusion), kind=kLoop, calls=%fused_computation.71 | loop fusion | flops 1048576 | bytes 4194560 | tf_op jit(solution)/shard_map/broadcast_in_dim | solution.py:115
  (10 shorter events, 0.1 us)
Async XLA Ops:
  0.6 5.6 %copy-start.4 = (s32[4096]{0:T(1024)S(1)}, s32[4096]{0:T(1024)}, u32[]{:S(2)}) copy-start(s32[4096]{0:T(1024)} %param.12) | copy-start | bytes 49156
  15.6 16.3 %copy-start.3 = (f32[16]{0:T(128)S(1)}, f32[16]{0:T(128)}, u32[]{:S(2)}) copy-start(f32[16]{0:T(128)} %param.13) | copy-start | bytes 196
  15.6 17.0 %copy-start.5 = (s32[256]{0:T(256)S(1)}, s32[256]{0:T(256)}, u32[]{:S(2)}) copy-start(s32[256]{0:T(256)} %param.14) | copy-start | bytes 3076
  23.2 33.7 %all-to-all-start = ((f32[32,1,256]{2,1,0:T(1,128)}), f32[32,1,256]{2,1,0:T(1,128)S(1)}, u32[]{:S(2)}, u32[]{:S(2)}) async-start(f32[32,1,256]{2,1,0:T(1,128)} %broadcast_in_dim.33), calls=%async_computation | async-start | bytes 65536 | tf_op jit(solution)/shard_map/all_to_all | solution.py:18
  85.5 45.9 %copy-start = (f32[1,8,4096]{2,1,0:T(8,128)S(1)}, f32[1,8,4096]{2,1,0:T(8,128)}, u32[]{:S(2)}) copy-start(f32[1,8,4096]{2,1,0:T(8,128)} %param.15) | copy-start | bytes 393220
  85.5 45.9 %copy-start.1 = (f32[1,8,4096]{2,1,0:T(8,128)S(1)}, f32[1,8,4096]{2,1,0:T(8,128)}, u32[]{:S(2)}) copy-start(f32[1,8,4096]{2,1,0:T(8,128)} %param.17) | copy-start | bytes 393220
  85.5 45.9 %copy-start.2 = (f32[1,8,4096]{2,1,0:T(8,128)S(1)}, f32[1,8,4096]{2,1,0:T(8,128)}, u32[]{:S(2)}) copy-start(f32[1,8,4096]{2,1,0:T(8,128)} %param.16) | copy-start | bytes 393220
  85.5 35.8 %all-to-all-start.1 = ((bf16[32,8,4096]{2,1,0:T(8,128)(2,1)}), bf16[32,8,4096]{2,1,0:T(8,128)(2,1)S(1)}, u32[]{:S(2)}, u32[]{:S(2)}) async-start(bf16[32,8,4096]{2,1,0:T(8,128)(2,1)} %select_bitcast_fusion.1), calls=%async_computation.1 | async-start | bytes 4194304 | tf_op jit(solution)/shard_map/all_to_all | solution.py:95
  133.1 32.9 %all-to-all-start.2 = ((bf16[32,8,4096]{2,1,0:T(8,128)(2,1)}), bf16[32,8,4096]{2,1,0:T(8,128)(2,1)S(1)}, u32[]{:S(2)}, u32[]{:S(2)}) async-start(bf16[32,8,4096]{2,1,0:T(8,128)(2,1)} %broadcast_in_dim.36), calls=%async_computation.2 | async-start | bytes 4194304 | tf_op jit(solution)/shard_map/all_to_all | solution.py:18
where the time goes:
time: 173 us; the launch traced here: 172 us
  waiting for transfers between devices  52.5 us (30%)
  other arithmetic  42.2 us (24%)
  local copies, waits for them, and re-layouts  23 us (13%)
  starting transfers between devices  20.6 us (12%)
  between operations  19.5 us (11%)
  matrix products  14.5 us (8%)
    all_to_all x1, waiting for transfers between devices, local(): lax.all_to_all(slotted.reshape(groups, owned, slotted.shape[1]), 'dp', sp...  28.2 us
    all_to_all x2, waiting for transfers between devices, from_everyone(): return lax.all_to_all(copies, axis, split_axis=0, concat_axis=0, tiled=True)  24.3 us
    convert_element_type x1, other arithmetic, local(): (encode(rotated / block_scale[:, None], levels) + offsets).astype(jnp.bfl...  20.1 us
    dot_general x4, matrix products, square_transform(): jnp.einsum('ac,ncd,db->nab', table, folded, table, precision=lax.Precisio...  14.5 us
    all_to_all x2, starting transfers between devices, from_everyone(): return lax.all_to_all(copies, axis, split_axis=0, concat_axis=0, tiled=True)  13.1 us
    reduce_sum x1, other arithmetic, local(): jnp.sum(decode(lax.all_to_all(slotted.reshape(groups, owned, slotted.shap...  8.95 us
    all_to_all x1, starting transfers between devices, local(): lax.all_to_all(slotted.reshape(groups, owned, slotted.shape[1]), 'dp', sp...  7.51 us
    div x1, local copies, waits for them, and re-layouts, square_transform(): return turned.reshape(blocks.shape) / edge_length  5.66 us
  transfers between devices with their start and end apart: 3, of which 2 were waited for; matrix products, arithmetic and copies ran while one was open for 6% of the time, Pallas kernels for 0%

commit v1 on v0

v1 whole, which is shorter than its diff:
```python
import functools

import jax
import jax.numpy as jnp
from jax import lax
from jax.experimental import pallas as pl
from jax.experimental.pallas import tpu as pltpu
from jax.sharding import Mesh, PartitionSpec as P

adam_epsilon = 1e-08
learning_rate = 0.02
weight_decay = 0.1
first_decay = 0.9
second_decay = 0.95
dither_steps = 256.0

LANES = 128
WIDE = 256
CELLS = 64
CELL_RATE = 31.95
VMEM_BYTES = 48 * 1024 * 1024
OTHER_CORE = ((0, 1), (1, 0))


def hadamard(edge):
    common = lax.broadcasted_iota(jnp.int32, (edge, edge), 0) & lax.broadcasted_iota(jnp.int32, (edge, edge), 1)
    parity = jnp.zeros((edge, edge), jnp.int32)
    for bit in range(edge.bit_length() - 1):
        parity = parity ^ ((common >> bit) & 1)
    return (1 - 2 * parity).astype(jnp.float32)


def three_pieces(values):
    high = values.astype(jnp.bfloat16)
    rest = values - high.astype(jnp.float32)
    middle = rest.astype(jnp.bfloat16)
    low = (rest - middle.astype(jnp.float32)).astype(jnp.bfloat16)
    return high, middle, low


def butterflies(parts):
    parts = list(parts)
    stride = 1
    while stride < len(parts):
        for first in range(len(parts)):
            if not first & stride:
                one, two = parts[first], parts[first + stride]
                parts[first], parts[first + stride] = one + two, one - two
        stride *= 2
    return parts


def times_table(values, table):
    pieces = jnp.concatenate(three_pieces(values), axis=1)
    return jnp.dot(pieces, table, preferred_element_type=jnp.float32)


def looked_up(table, index):
    return jnp.take_along_axis(table, index, axis=1)


def rotate_kernel(gradient_ref, bits_ref, rotated_ref, peaks_ref, table_ref, rows_ref):
    step = pl.program_id(0)
    rows, block = gradient_ref.shape

    @pl.when(step == 0)
    def _():
        table = (hadamard(WIDE) * (1.0 / 64.0)).astype(jnp.bfloat16)
        for piece in range(3):
            table_ref[pl.ds(piece * WIDE, WIDE), :] = table

    flips = (1 - 2 * bits_ref[...]).astype(jnp.float32)
    parts = butterflies(
        gradient_ref[:, at : at + WIDE] * flips[:, at : at + WIDE] for at in range(0, block, WIDE)
    )
    most = jnp.zeros((rows, WIDE), jnp.float32)
    for number, part in enumerate(parts):
        turned = times_table(part, table_ref[...])
        rotated_ref[:, number * WIDE : (number + 1) * WIDE] = turned
        most = jnp.maximum(most, jnp.abs(turned))
    rows_ref[pl.ds(pl.multiple_of(step * rows, rows), rows), :] = jnp.maximum(most[:, :LANES], most[:, LANES:])

    @pl.when(step == pl.num_programs(0) - 1)
    def _():
        blocks = rows_ref.shape[0]
        lines = [
            jnp.max(jnp.transpose(rows_ref[at : at + LANES, :]), axis=0, keepdims=True) for at in range(0, blocks, LANES)
        ]
        lines = jnp.concatenate(lines * (8 // len(lines)), axis=0)
        peaks_ref[...] = jnp.broadcast_to(lines[None], peaks_ref.shape)


def rotate(gradient, bits, groups):
    blocks, block = gradient.shape
    rows = 32
    return pl.pallas_call(
        rotate_kernel,
        grid=(blocks // rows,),
        in_specs=[
            pl.BlockSpec((rows, block), lambda i: (i, 0)),
            pl.BlockSpec((1, block), lambda i: (0, 0)),
        ],
        out_specs=[
            pl.BlockSpec((rows, block), lambda i: (i, 0)),
            pl.BlockSpec((groups, 8, LANES), lambda i: (0, 0, 0)),
        ],
        out_shape=[
            jax.ShapeDtypeStruct((blocks, block), jnp.float32),
            jax.ShapeDtypeStruct((groups, 8, LANES), jnp.float32),
        ],
        scratch_shapes=[pltpu.VMEM((3 * WIDE, WIDE), jnp.bfloat16), pltpu.VMEM((blocks, LANES), jnp.float32)],
        compiler_params=pltpu.CompilerParams(vmem_limit_bytes=VMEM_BYTES),
        name="rotate",
    )(gradient, bits)


def encode_tables(levels_ref):
    count = levels_ref.shape[0]
    lane = lax.broadcasted_iota(jnp.int32, (8, LANES), 1)
    cell = lane & (CELLS - 1)
    threshold = jnp.full((8, LANES), 4.0, jnp.float32)
    position = jnp.zeros((8, LANES), jnp.int32)
    for number in range(1, count - 1):
        level = jnp.full((8, LANES), levels_ref[number], jnp.float32)
        its_cell = (level * CELL_RATE + 32.0).astype(jnp.int32)
        threshold = jnp.where(its_cell == cell, level, threshold)
        before = (its_cell < cell) | ((its_cell == cell) & (lane >= CELLS))
        position = position + before.astype(jnp.int32)
    slope = jnp.zeros((8, LANES), jnp.float32)
    intercept = jnp.zeros((8, LANES), jnp.float32)
    for number in range(count - 1):
        low = jnp.full((8, LANES), levels_ref[number], jnp.float32)
        high = jnp.full((8, LANES), levels_ref[number + 1], jnp.float32)
        its_slope = 1.0 / (high - low)
        its_intercept = (number + (0.5 / dither_steps - 0.5)) - low * its_slope
        slope = jnp.where(position == number, its_slope, slope)
        intercept = jnp.where(position == number, its_intercept, intercept)
    return threshold, slope, intercept


def decode_tables(levels_ref):
    count = levels_ref.shape[0]
    lane = lax.broadcasted_iota(jnp.int32, (8, LANES), 1)
    slope = jnp.zeros((8, LANES), jnp.float32)
    intercept = jnp.full((8, LANES), levels_ref[count - 1], jnp.float32)
    for number in range(count - 1):
        low = jnp.full((8, LANES), levels_ref[number], jnp.float32)
        high = jnp.full((8, LANES), levels_ref[number + 1], jnp.float32)
        slope = jnp.where(lane == number, high - low, slope)
        intercept = jnp.where(lane == number, low - number * (high - low), intercept)
    return slope, intercept


def encode_kernel(levels_ref, rotated_ref, dither_ref, peaks_ref, layout_ref, symbols_ref, scales_ref, inverse_ref, order_ref, held_ref):
    step = pl.program_id(0)
    blocks, columns = rotated_ref.shape

    @pl.when(step == 0)
    def _():
        lines = jnp.max(peaks_ref[...], axis=0) + 1e-06
        wide = jnp.concatenate([lines[i : i + 1, :] for i in range(blocks // LANES)], axis=1)
        order = lax.broadcasted_iota(jnp.int32, (blocks, blocks), 0) == layout_ref[...]
        order = jnp.transpose(order.astype(jnp.float32))
        order_ref[...] = order.astype(jnp.bfloat16)
        slot = jnp.sum(jnp.where(order > 0.5, wide, 0.0), axis=1, keepdims=True)
        scales_ref[...] = jnp.broadcast_to(slot, (blocks, LANES))
        for at in range(blocks // LANES):
            square = jnp.broadcast_to(lines[at : at + 1, :], (LANES, LANES))
            inverse_ref[at * LANES : (at + 1) * LANES, :] = 1.0 / jnp.transpose(square)

    threshold, slope, intercept = encode_tables(levels_ref)

    def eight_rows(number, carry):
        at = pl.multiple_of(number * 16, 16)
        for part in range(columns // LANES):
            pair = []
            for half in range(2):
                here = pl.ds(pl.multiple_of(at + half * 8, 8), 8)
                over = slice(part * LANES, (part + 1) * LANES)
                ratio = rotated_ref[here, over] * inverse_ref[here, :]
                cell = (ratio * CELL_RATE + 32.0).astype(jnp.int32)
                side = jnp.where(ratio >= looked_up(threshold, cell), cell + CELLS, cell)
                value = ratio * looked_up(slope, side) + looked_up(intercept, side)
                pair.append(value + dither_ref[here, over].astype(jnp.float32) * (1.0 / dither_steps))
            held_ref[pl.ds(at, 16), part * LANES : (part + 1) * LANES] = jnp.concatenate(pair, axis=0).astype(jnp.bfloat16)
        return carry

    lax.fori_loop(0, blocks // 16, eight_rows, 0)
    slotted = jnp.dot(order_ref[...], held_ref[...], preferred_element_type=jnp.float32)
    symbols_ref[...] = slotted.astype(jnp.bfloat16)


def encode(rotated, dither, peaks, layout, levels):
    blocks, block = rotated.shape
    columns = 512
    return pl.pallas_call(
        encode_kernel,
        grid=(block // columns,),
        in_specs=[
            pl.BlockSpec(memory_space=pltpu.SMEM),
            pl.BlockSpec((blocks, columns), lambda i: (0, i)),
            pl.BlockSpec((blocks, columns), lambda i: (0, i)),
            pl.BlockSpec(peaks.shape, lambda i: (0, 0, 0)),
            pl.BlockSpec((1, blocks), lambda i: (0, 0)),
        ],
        out_specs=[
            pl.BlockSpec((blocks, columns), lambda i: (0, i)),
            pl.BlockSpec((blocks, LANES), lambda i: (0, 0)),
        ],
        out_shape=[
            jax.ShapeDtypeStruct((blocks, block), jnp.bfloat16),
            jax.ShapeDtypeStruct((blocks, LANES), jnp.float32),
        ],
        scratch_shapes=[
            pltpu.VMEM((blocks, LANES), jnp.float32),
            pltpu.VMEM((blocks, blocks), jnp.bfloat16),
            pltpu.VMEM((blocks, columns), jnp.bfloat16),
        ],
        compiler_params=pltpu.CompilerParams(vmem_limit_bytes=VMEM_BYTES),
        name="encode",
    )(levels, rotated, dither, peaks, layout)


def owner_kernel(
    first_ref, levels_ref, symbols_ref, scales_ref, bits_ref, master_ref, moment_ref, second_ref,
    new_master_ref, new_moment_ref, new_second_ref, copies_ref, total_ref, table_ref,
):
    step = pl.program_id(0)
    rows, block = total_ref.shape
    count = levels_ref.shape[0]
    slope, intercept = decode_tables(levels_ref)

    @pl.when(step == 0)
    def _():
        total_ref[...] = jnp.zeros_like(total_ref)
        table = (hadamard(WIDE) * (1.0 / 64.0)).astype(jnp.bfloat16)
        for piece in range(3):
            table_ref[pl.ds(piece * WIDE, WIDE), :] = table

    def column(number, carry):
        over = pl.ds(pl.multiple_of(number * LANES, LANES), LANES)
        total = total_ref[:, over]
        for replica in range(symbols_ref.shape[0]):
            symbol = symbols_ref[replica, :, over].astype(jnp.float32)
            symbol = jnp.minimum(jnp.maximum(symbol, 0.0), count - 1.0)
            number_of = symbol.astype(jnp.int32)
            total = total + (symbol * looked_up(slope, number_of) + looked_up(intercept, number_of))
        total_ref[:, over] = total
        return carry

    lax.fori_loop(0, block // LANES, column, 0)

    @pl.when(step == pl.num_programs(0) - 1)
    def _():
        flips = (1 - 2 * bits_ref[...]).astype(jnp.float32)
        scales = jnp.concatenate([scales_ref[...]] * (WIDE // LANES), axis=1)
        parts = butterflies(total_ref[:, at : at + WIDE] * scales for at in range(0, block, WIDE))
        for number, part in enumerate(parts):
            over = slice(number * WIDE, (number + 1) * WIDE)
            grads = times_table(part, table_ref[...]) * flips[:, over]
            moment = first_decay * moment_ref[:, over] + (1.0 - first_decay) * grads
            second = second_decay * second_ref[:, over] + (1.0 - second_decay) * grads * grads
            master = master_ref[:, over]
            updated = master - learning_rate * (moment / (jnp.sqrt(second) + adam_epsilon) + weight_decay * master)
            new_moment_ref[:, over] = moment
            new_second_ref[:, over] = second
            new_master_ref[:, over] = updated
            rounded = updated.astype(jnp.bfloat16)
            for copy in range(copies_ref.shape[0]):
                copies_ref[copy, :, over] = rounded


def owner(place, levels, received, scales, bits, master, moment, second, copies):
    replicas, rows, block = received.shape
    each = 8
    whole = pl.BlockSpec((rows, block), lambda i, place: (0, 0))
    return pl.pallas_call(
        owner_kernel,
        grid_spec=pltpu.PrefetchScalarGridSpec(
            num_scalar_prefetch=1,
            grid=(replicas // each,),
            in_specs=[
                pl.BlockSpec(memory_space=pltpu.SMEM),
                pl.BlockSpec((each, rows, block), lambda i, place: (i, 0, 0)),
                pl.BlockSpec((rows, LANES), lambda i, place: (place[0], 0)),
                pl.BlockSpec((1, block), lambda i, place: (0, 0)),
                whole,
                whole,
                whole,
            ],
            out_specs=[whole, whole, whole, pl.BlockSpec((copies, rows, block), lambda i, place: (0, 0, 0))],
            scratch_shapes=[pltpu.VMEM((rows, block), jnp.float32), pltpu.VMEM((3 * WIDE, WIDE), jnp.bfloat16)],
        ),
        out_shape=[jax.ShapeDtypeStruct((rows, block), jnp.float32)] * 3
        + [jax.ShapeDtypeStruct((copies, rows, block), jnp.bfloat16)],
        compiler_params=pltpu.CompilerParams(vmem_limit_bytes=VMEM_BYTES),
        name="owner",
    )(place, levels, received, scales, bits, master, moment, second)


def reorder_kernel(mine_ref, others_ref, my_slots_ref, other_slots_ref, out_ref):
    blocks = out_ref.shape[0]
    half = mine_ref.shape[0]
    row = lax.broadcasted_iota(jnp.int32, (blocks, half), 0)
    my_order = (row == my_slots_ref[...]).astype(jnp.float32).astype(jnp.bfloat16)
    other_order = (row == other_slots_ref[...]).astype(jnp.float32).astype(jnp.bfloat16)
    order = jnp.concatenate([my_order, other_order], axis=1)
    held = jnp.concatenate([mine_ref[...], others_ref[...]], axis=0)
    out_ref[...] = jnp.dot(order, held, preferred_element_type=jnp.float32).astype(jnp.bfloat16)


def reorder(mine, others, my_slots, other_slots):
    half, block = mine.shape
    columns = 1024
    return pl.pallas_call(
        reorder_kernel,
        grid=(block // columns,),
        in_specs=[
            pl.BlockSpec((half, columns), lambda i: (0, i)),
            pl.BlockSpec((half, columns), lambda i: (0, i)),
            pl.BlockSpec((1, half), lambda i: (0, 0)),
            pl.BlockSpec((1, half), lambda i: (0, 0)),
        ],
        out_specs=pl.BlockSpec((2 * half, columns), lambda i: (0, i)),
        out_shape=jax.ShapeDtypeStruct((2 * half, block), jnp.bfloat16),
        compiler_params=pltpu.CompilerParams(vmem_limit_bytes=VMEM_BYTES),
        name="reorder",
    )(mine, others, my_slots, other_slots)


def local(axes, gradient, dither, sign_bits, levels, layout, master, first_moment, second_moment):
    groups = lax.axis_size(axes)
    chips, core = axes[:-1], axes[-1]
    blocks, block = gradient.shape[2:]
    owned = blocks // groups
    bits = sign_bits.reshape(1, block)
    rotated, peaks = rotate(gradient[0, 0], bits, groups)
    peaks = lax.all_to_all(peaks, axes, 0, 0, tiled=True)
    symbols, scales = encode(rotated, dither[0, 0], peaks, layout.reshape(1, blocks), levels)
    received = lax.all_to_all(symbols.reshape(groups, owned, block), axes, 0, 0, tiled=True)
    place = lax.axis_index(axes).reshape(1)
    new_master, new_moment, new_second, copies = owner(
        place, levels, received, scales, bits, master[0], first_moment[0], second_moment[0], groups // 2
    )
    mine = lax.all_to_all(copies, chips, 0, 0, tiled=True)
    others = lax.ppermute(mine, core, OTHER_CORE)
    by_core = layout.reshape(groups // 2, 2, owned)
    which = lax.axis_index(core)
    my_slots = lax.dynamic_index_in_dim(by_core, which, 1, False).reshape(1, blocks // 2)
    other_slots = lax.dynamic_index_in_dim(by_core, 1 - which, 1, False).reshape(1, blocks // 2)
    parameters = reorder(
        mine.reshape(blocks // 2, block), others.reshape(blocks // 2, block), my_slots, other_slots
    )
    return (new_master[None], new_moment[None], new_second[None], parameters[None])


def solution(mesh):
    section, dp = mesh.axis_names
    axes = ("dp_chip", "dp_core")
    split = Mesh(mesh.devices.reshape(mesh.shape[section], mesh.shape[dp] // 2, 2), (section, *axes))
    placed = (
        P(section, axes, None, None),
        P(section, axes, None, None),
        P(),
        P(),
        P(),
        P(section, axes, None),
        P(section, axes, None),
        P(section, axes, None),
    )
    return jax.shard_map(
        functools.partial(local, axes),
        mesh=split,
        in_specs=placed,
        out_specs=(P(section, axes, None), P(section, axes, None), P(section, axes, None), P(section, None, None)),
        check_vma=False,
    )
```

time: 173 us -> 135 us (0.78)
  Pallas kernels: 0 us -> 58.2 us
  other arithmetic: 42.2 us -> 0 us
  blocking collectives: 0 us -> 34.6 us
  waiting for transfers between devices: 52.5 us -> 30.3 us
  between operations: 19.5 us -> 0.75 us
  local copies, waits for them, and re-layouts: 23 us -> 4.32 us
  matrix products: 14.5 us -> 0 us
  starting transfers between devices: 20.6 us -> 6.13 us
    pallas_call x0 -> x4, Pallas kernels: none -> 58.2 us  [the longest x1 28.3 us: encode(): pl.pallas_call(encode_kernel, grid=(block // columns,), in_specs=[pl.Bloc...]
    all_to_all x0 -> x2, blocking collectives: none -> 34.6 us  [the longest x1 18.6 us: local(): mine = lax.all_to_all(copies, chips, 0, 0, tiled=True)]
    all_to_all x3 -> x1, waiting for transfers between devices: 52.5 us -> 28.4 us  [local(): lax.all_to_all(symbols.reshape(groups, owned, block), axes, 0, 0, tiled=T...]
    convert_element_type x3 -> x0, other arithmetic: 20.3 us -> none  [the longest x1 20.1 us: local(): (encode(rotated / block_scale[:, None], levels) + offsets).astype(jnp.bfl...]
    all_to_all x3 -> x1, starting transfers between devices: 20.6 us -> 4.21 us  [local(): lax.all_to_all(symbols.reshape(groups, owned, block), axes, 0, 0, tiled=T...]
    dot_general x4 -> x0, matrix products: 14.5 us -> none  [square_transform(): jnp.einsum('ac,ncd,db->nab', table, folded, table, precision=lax.Precisio...]
    reduce_sum x1 -> x0, other arithmetic: 8.95 us -> none  [local(): jnp.sum(decode(lax.all_to_all(slotted.reshape(groups, owned, slotted.shap...]
    gather x3 -> x0, local copies, waits for them, and re-layouts: 8.28 us -> none  [the longest x1 3.17 us: local(): slotted = jnp.take(symbols, layout, axis=0)]
  transfers between devices with their start and end apart: 3 -> 2, of which waited for: 2 -> 2; matrix products, arithmetic and copies ran while one was open for 6% -> 0% of each run, Pallas kernels for 0% -> 0%
where the time goes in v1:
time: 135 us; the launch traced here: 134 us
  Pallas kernels  58.2 us (43%)
  blocking collectives  34.6 us (26%)
  waiting for transfers between devices  30.3 us (22%)
  starting transfers between devices  6.13 us (5%)
  local copies, waits for them, and re-layouts  4.32 us (3%)
    all_to_all x1, waiting for transfers between devices, local(): lax.all_to_all(symbols.reshape(groups, owned, block), axes, 0, 0, tiled=T...  28.4 us
    pallas_call x1, Pallas kernels, encode(): pl.pallas_call(encode_kernel, grid=(block // columns,), in_specs=[pl.Bloc...  28.3 us
    all_to_all x1, blocking collectives, local(): mine = lax.all_to_all(copies, chips, 0, 0, tiled=True)  18.6 us
    pallas_call x1, Pallas kernels, owner(): pl.pallas_call(owner_kernel, grid_spec=pltpu.PrefetchScalarGridSpec(num_s...  16.7 us
    all_to_all x1, blocking collectives, local(): peaks = lax.all_to_all(peaks, axes, 0, 0, tiled=True)  16.1 us
    pallas_call x1, Pallas kernels, rotate(): pl.pallas_call(rotate_kernel, grid=(blocks // rows,), in_specs=[pl.BlockS...  10.5 us
    all_to_all x1, starting transfers between devices, local(): lax.all_to_all(symbols.reshape(groups, owned, block), axes, 0, 0, tiled=T...  4.21 us
    unnamed x18, local copies, waits for them, and re-layouts  4 us
  transfers between devices with their start and end apart: 2, of which 2 were waited for; matrix products, arithmetic and copies ran while one was open for 0% of the time, Pallas kernels for 0%

profile of v1, /device:TPU:1, one launch (start us, length us, event | category | flops | bytes accessed | tf_op | source)
XLA Modules:
  0.0 134.4 jit_solution(7106588953999824760)
XLA Ops:
  0.6 0.0 copy-start.8
  0.6 0.0 copy-start.7
  0.7 0.0 copy-start.5
  0.7 0.7 copy-done.5
  1.4 10.5 %rotate.1 = (f32[256,4096]{1,0:T(8,128)S(1)}, f32[32,8,128]{2,1,0:T(8,128)S(1)}) custom-call(f32[256,4096]{1,0:T(8,128)} %bitcast.24, s32[1,4096]{1,0:T(1,128)S(1)} %bitcast.21), custom_call_target="tpu_custom_call" | custom-call | tf_op jit(solution)/shard_map/rotate/pallas_call | solution.py:96
  11.9 0.0 copy-start
  11.9 1.9 %copy-done = f32[256,4096]{1,0:T(8,128)} copy-done((f32[256,4096]{1,0:T(8,128)}, f32[256,4096]{1,0:T(8,128)S(1)}, u32[]{:S(2)}) %copy-start) | copy-done | bytes 4194328
  13.9 16.1 %all_to_all.15.peaks_ref = f32[32,8,128]{2,1,0:T(8,128)S(1)} all-to-all(f32[32,8,128]{2,1,0:T(8,128)S(1)} %get-tuple-element.13), channel_id=1, replica_groups=mesh['section'=4,'dp_chip'=16,'dp_core'=2] {'dp_chip','dp_core'}, dimensions={0} | all-to-all | bytes 262144 | tf_op jit(solution)/shard_map/all_to_all | solution.py:338
  29.9 0.0 copy-done.8
  29.9 0.0 copy-done.7
  30.0 28.3 %encode.1 = (bf16[256,4096]{1,0:T(8,128)(2,1)S(1)}, f32[256,128]{1,0:T(8,128)S(1)}) custom-call(f32[16]{0:T(128)S(1)} %copy-done.8, f32[256,4096]{1,0:T(8,128)} %copy-done, s32[256,4096]{1,0:T(8,128)} %bitcast.25, f32[32,8,128]{2,1,0:T(8,128)S(1)} %all_to_all.15.peaks_ref, s32[1,256]{1,0:T(1,128)S(1)} %bitcast.23), custom_call_target="tpu_custom_call" | custom-call | tf_op jit(solution)/shard_map/encode/pallas_call | solution.py:196
  58.3 0.0 copy-start.1
  58.3 1.3 copy-done.1
  59.6 0.0 copy-start.2
  59.6 0.0 copy-start.3
  59.6 0.0 copy-start.4
  59.6 0.0 copy-start.6
  59.6 4.2 %all-to-all-start.1 = ((bf16[32,8,4096]{2,1,0:T(8,128)(2,1)}), bf16[32,8,4096]{2,1,0:T(8,128)(2,1)S(1)}, u32[]{:S(2)}, u32[]{:S(2)}) async-start(bf16[32,8,4096]{2,1,0:T(8,128)(2,1)} %bitcast.16), calls=%async_computation.1 | async-start | bytes 4194304 | tf_op jit(solution)/shard_map/all_to_all | solution.py:340
  63.9 28.4 %all-to-all-done.1.symbols_ref = bf16[32,8,4096]{2,1,0:T(8,128)(2,1)S(1)} async-done(((bf16[32,8,4096]{2,1,0:T(8,128)(2,1)}), bf16[32,8,4096]{2,1,0:T(8,128)(2,1)S(1)}, u32[]{:S(2)}, u32[]{:S(2)}) %all-to-all-start.1) | async-done | bytes 2097184 | tf_op jit(solution)/shard_map/all_to_all | solution.py:340
  92.2 0.0 copy-done.2
  92.2 0.0 copy-done.3
  92.2 0.0 copy-done.4
  92.2 0.0 copy-done.6
  92.2 16.7 %owner.1 = (f32[8,4096]{1,0:T(8,128)}, f32[8,4096]{1,0:T(8,128)}, f32[8,4096]{1,0:T(8,128)}, bf16[16,8,4096]{2,1,0:T(8,128)(2,1)S(1)}) custom-call(s32[1]{0:T(128)} %bitcast.first_ref, f32[16]{0:T(128)S(1)} %copy-done.8, bf16[32,8,4096]{2,1,0:T(8,128)(2,1)S(1)} %all-to-all-done.1.symbols_ref, f32[256,128]{1,0:T(8,128)S(1)} %get-tuple-element.15.scales_ref, ...), custom_call_target="tpu_custom_call" | custom-call | tf_op jit(solution)/shard_map/owner/pallas_call | solution.py:277
  109.0 18.6 %all_to_all.16 = bf16[16,8,4096]{2,1,0:T(8,128)(2,1)S(1)} all-to-all(bf16[16,8,4096]{2,1,0:T(8,128)(2,1)S(1)} %get-tuple-element.19), channel_id=1, replica_groups=mesh['section'=4,'dp_chip'=16,'dp_core'=2] {'dp_chip'}, dimensions={0} | all-to-all | bytes 2097152 | tf_op jit(solution)/shard_map/all_to_all | solution.py:345
  127.6 1.9 %collective-permute-start = (bf16[16,8,4096]{2,1,0:T(8,128)(2,1)S(1)}, bf16[16,8,4096]{2,1,0:T(8,128)(2,1)S(1)}, u32[]{:S(2)}, u32[]{:S(2)}) collective-permute-start(bf16[16,8,4096]{2,1,0:T(8,128)(2,1)S(1)} %all_to_all.16), channel_id=1, source_target_pairs={{0,1},{1,0},{2,3},{3,2},{4,5},{5,4},{6,7},{7,6},{8,9},{9,8},{10,11... | collective-permute-start | bytes 3145736 | tf_op jit(solution)/shard_map/ppermute | solution.py:346
  129.5 0.1 reshape.43
  129.6 0.1 dynamic-slice_reduce_fusion
  129.6 0.1 reshape.44.my_slots_ref
  129.7 0.1 reshape.45.other_slots_ref
  129.8 1.9 %collective-permute-done = bf16[16,8,4096]{2,1,0:T(8,128)(2,1)S(1)} collective-permute-done((bf16[16,8,4096]{2,1,0:T(8,128)(2,1)S(1)}, bf16[16,8,4096]{2,1,0:T(8,128)(2,1)S(1)}, u32[]{:S(2)}, u32[]{:S(2)}) %collective-permute-start) | collective-permute-done | bytes 1048608 | tf_op jit(solution)/shard_map/ppermute | solution.py:346
  131.8 2.6 %reorder.1 = bf16[256,4096]{1,0:T(8,128)(2,1)} custom-call(bf16[128,4096]{1,0:T(8,128)(2,1)S(1)} %bitcast.15, bf16[128,4096]{1,0:T(8,128)(2,1)S(1)} %bitcast.17, s32[1,128]{1,0:T(1,128)S(1)} %reshape.44.my_slots_ref, s32[1,128]{1,0:T(1,128)S(1)} %reshape.45.other_slots_ref), custom_call_target="tpu_custom_call" | custom-call | tf_op jit(solution)/shard_map/reorder/pallas_call | solution.py:315
Async XLA Ops:
  0.6 29.3 %copy-start.8 = (f32[16]{0:T(128)S(1)}, f32[16]{0:T(128)}, u32[]{:S(2)}) copy-start(f32[16]{0:T(128)} %levels_ref.3) | copy-start | bytes 196
  0.6 29.3 %copy-start.7 = (s32[256]{0:T(256)S(1)}, s32[256]{0:T(256)}, u32[]{:S(2)}) copy-start(s32[256]{0:T(256)} %param.12) | copy-start | bytes 3076
  0.7 0.7 copy-start.5
  11.9 1.9 %copy-start = (f32[256,4096]{1,0:T(8,128)}, f32[256,4096]{1,0:T(8,128)S(1)}, u32[]{:S(2)}) copy-start(f32[256,4096]{1,0:T(8,128)S(1)} %get-tuple-element.12.rotated_ref) | copy-start | bytes 12582916
  58.3 1.3 copy-start.1
  59.6 32.6 %copy-start.2 = (f32[1,8,4096]{2,1,0:T(8,128)S(1)}, f32[1,8,4096]{2,1,0:T(8,128)}, u32[]{:S(2)}) copy-start(f32[1,8,4096]{2,1,0:T(8,128)} %param.13) | copy-start | bytes 393220
  59.6 32.6 %copy-start.3 = (f32[1,8,4096]{2,1,0:T(8,128)S(1)}, f32[1,8,4096]{2,1,0:T(8,128)}, u32[]{:S(2)}) copy-start(f32[1,8,4096]{2,1,0:T(8,128)} %param.14) | copy-start | bytes 393220
  59.6 32.6 %copy-start.4 = (f32[1,8,4096]{2,1,0:T(8,128)S(1)}, f32[1,8,4096]{2,1,0:T(8,128)}, u32[]{:S(2)}) copy-start(f32[1,8,4096]{2,1,0:T(8,128)} %param.15) | copy-start | bytes 393220
  59.6 32.6 %copy-start.6 = (s32[4096]{0:T(1024)S(1)}, s32[4096]{0:T(1024)}, u32[]{:S(2)}) copy-start(s32[4096]{0:T(1024)} %param.10) | copy-start | bytes 49156
  59.6 32.6 %all-to-all-start.1 = ((bf16[32,8,4096]{2,1,0:T(8,128)(2,1)}), bf16[32,8,4096]{2,1,0:T(8,128)(2,1)S(1)}, u32[]{:S(2)}, u32[]{:S(2)}) async-start(bf16[32,8,4096]{2,1,0:T(8,128)(2,1)} %bitcast.16), calls=%async_computation.1 | async-start | bytes 4194304 | tf_op jit(solution)/shard_map/all_to_all | solution.py:340
  127.6 4.2 %collective-permute-start = (bf16[16,8,4096]{2,1,0:T(8,128)(2,1)S(1)}, bf16[16,8,4096]{2,1,0:T(8,128)(2,1)S(1)}, u32[]{:S(2)}, u32[]{:S(2)}) collective-permute-start(bf16[16,8,4096]{2,1,0:T(8,128)(2,1)S(1)} %all_to_all.16), channel_id=1, source_target_pairs={{0,1},{1,0},{2,3},{3,2},{4,5},{5,4},{6,7},{7,6},{8,9},{9,8},{10,11... | collective-permute-start | bytes 3145736 | tf_op jit(solution)/shard_map/ppermute | solution.py:346

commit v2 on v1

--- a/solution.py
+++ b/solution.py
@@ -18,7 +18,8 @@
 WIDE = 256
 CELLS = 64
 CELL_RATE = 31.95
-VMEM_BYTES = 48 * 1024 * 1024
+MIB = 1024 * 1024
+VMEM_BYTES = 16 * MIB
 OTHER_CORE = ((0, 1), (1, 0))
 
 
@@ -55,8 +56,17 @@
     return jnp.dot(pieces, table, preferred_element_type=jnp.float32)
 
 
+BY_LANE = lax.GatherDimensionNumbers(
+    offset_dims=(),
+    collapsed_slice_dims=(1,),
+    start_index_map=(1,),
+    operand_batching_dims=(0,),
+    start_indices_batching_dims=(0,),
+)
+
+
 def looked_up(table, index):
-    return jnp.take_along_axis(table, index, axis=1)
+    return lax.gather(table, index[..., None], BY_LANE, (1, 1), mode=lax.GatherScatterMode.PROMISE_IN_BOUNDS)
 
 
 def rotate_kernel(gradient_ref, bits_ref, rotated_ref, peaks_ref, table_ref, rows_ref):
@@ -70,14 +80,13 @@
             table_ref[pl.ds(piece * WIDE, WIDE), :] = table
 
     flips = (1 - 2 * bits_ref[...]).astype(jnp.float32)
-    parts = butterflies(
-        gradient_ref[:, at : at + WIDE] * flips[:, at : at + WIDE] for at in range(0, block, WIDE)
-    )
+    parts = butterflies(gradient_ref[:, at : at + WIDE] * flips[:, at : at + WIDE] for at in range(0, block, WIDE))
+    turned = times_table(jnp.concatenate(parts, axis=0), table_ref[...])
     most = jnp.zeros((rows, WIDE), jnp.float32)
-    for number, part in enumerate(parts):
-        turned = times_table(part, table_ref[...])
-        rotated_ref[:, number * WIDE : (number + 1) * WIDE] = turned
-        most = jnp.maximum(most, jnp.abs(turned))
+    for number in range(block // WIDE):
+        part = turned[number * rows : (number + 1) * rows]
+        rotated_ref[:, number * WIDE : (number + 1) * WIDE] = part
+        most = jnp.maximum(most, jnp.abs(part))
     rows_ref[pl.ds(pl.multiple_of(step * rows, rows), rows), :] = jnp.maximum(most[:, :LANES], most[:, LANES:])
 
     @pl.when(step == pl.num_programs(0) - 1)
@@ -92,7 +101,7 @@
 
 def rotate(gradient, bits, groups):
     blocks, block = gradient.shape
-    rows = 32
+    rows = 64
     return pl.pallas_call(
         rotate_kernel,
         grid=(blocks // rows,),
@@ -109,7 +118,7 @@
             jax.ShapeDtypeStruct((groups, 8, LANES), jnp.float32),
         ],
         scratch_shapes=[pltpu.VMEM((3 * WIDE, WIDE), jnp.bfloat16), pltpu.VMEM((blocks, LANES), jnp.float32)],
-        compiler_params=pltpu.CompilerParams(vmem_limit_bytes=VMEM_BYTES),
+        compiler_params=pltpu.CompilerParams(vmem_limit_bytes=49 * MIB),
         name="rotate",
     )(gradient, bits)
 
@@ -138,22 +147,22 @@
     return threshold, slope, intercept
 
 
-def decode_tables(levels_ref):
-    count = levels_ref.shape[0]
-    lane = lax.broadcasted_iota(jnp.int32, (8, LANES), 1)
-    slope = jnp.zeros((8, LANES), jnp.float32)
-    intercept = jnp.full((8, LANES), levels_ref[count - 1], jnp.float32)
-    for number in range(count - 1):
+def line_tables(levels_ref):
+    lines = []
+    for number in range(levels_ref.shape[0] - 1):
         low = jnp.full((8, LANES), levels_ref[number], jnp.float32)
-        high = jnp.full((8, LANES), levels_ref[number + 1], jnp.float32)
-        slope = jnp.where(lane == number, high - low, slope)
-        intercept = jnp.where(lane == number, low - number * (high - low), intercept)
-    return slope, intercept
-
-
-def encode_kernel(levels_ref, rotated_ref, dither_ref, peaks_ref, layout_ref, symbols_ref, scales_ref, inverse_ref, order_ref, held_ref):
+        slope = 1.0 / (jnp.full((8, LANES), levels_ref[number + 1], jnp.float32) - low)
+        lines.append((slope, (number + (0.5 / dither_steps - 0.5)) - low * slope))
+    return lines
+
+
+def encode_kernel(
+    levels_ref, rotated_ref, dither_ref, peaks_ref, layout_ref, symbols_ref, scales_ref,
+    inverse_ref, order_ref, held_ref, tables_ref, lines_ref, out_ref, out_sems,
+):
     step = pl.program_id(0)
     blocks, columns = rotated_ref.shape
+    count = levels_ref.shape[0]
 
     @pl.when(step == 0)
     def _():
@@ -167,32 +176,74 @@
         for at in range(blocks // LANES):
             square = jnp.broadcast_to(lines[at : at + 1, :], (LANES, LANES))
             inverse_ref[at * LANES : (at + 1) * LANES, :] = 1.0 / jnp.transpose(square)
-
-    threshold, slope, intercept = encode_tables(levels_ref)
-
-    def eight_rows(number, carry):
-        at = pl.multiple_of(number * 16, 16)
+        for number, table in enumerate(encode_tables(levels_ref)):
+            tables_ref[number] = table
+        for number, (slope, intercept) in enumerate(line_tables(levels_ref)):
+            lines_ref[2 * number] = slope
+            lines_ref[2 * number + 1] = intercept
+
+    threshold, slope, intercept = tables_ref[0], tables_ref[1], tables_ref[2]
+    deep = 64
+
+    def some_rows(number, carry):
+        start = pl.multiple_of(number * deep, deep)
+        tiles = [(row, part) for part in range(columns // LANES) for row in range(0, deep, 8)]
+
+        def over(row, part, height=8):
+            return pl.ds(pl.multiple_of(start + row, height), height), slice(part * LANES, (part + 1) * LANES)
+
+        ratios = {tile: rotated_ref[over(*tile)] * inverse_ref[over(tile[0], 0)] for tile in tiles}
+        by_table = tiles[1::2]
+        cells = {tile: (ratios[tile] * CELL_RATE + 32.0).astype(jnp.int32) for tile in by_table}
+        limits = {tile: looked_up(threshold, cells[tile]) for tile in by_table}
+        sides = {
+            tile: jnp.where(ratios[tile] >= limits[tile], cells[tile] + CELLS, cells[tile]) for tile in by_table
+        }
+        slopes = {tile: looked_up(slope, sides[tile]) for tile in by_table}
+        intercepts = {tile: looked_up(intercept, sides[tile]) for tile in by_table}
+        values = {}
+        for tile in tiles:
+            ratio = ratios[tile]
+            if tile in slopes:
+                value = ratio * slopes[tile] + intercepts[tile]
+            else:
+                its_slope, its_intercept = lines_ref[0], lines_ref[1]
+                for level in range(1, count - 1):
+                    above = ratio >= levels_ref[level]
+                    its_slope = jnp.where(above, lines_ref[2 * level], its_slope)
+                    its_intercept = jnp.where(above, lines_ref[2 * level + 1], its_intercept)
+                value = ratio * its_slope + its_intercept
+            values[tile] = value + dither_ref[over(*tile)].astype(jnp.float32) * (1.0 / dither_steps)
         for part in range(columns // LANES):
-            pair = []
-            for half in range(2):
-                here = pl.ds(pl.multiple_of(at + half * 8, 8), 8)
-                over = slice(part * LANES, (part + 1) * LANES)
-                ratio = rotated_ref[here, over] * inverse_ref[here, :]
-                cell = (ratio * CELL_RATE + 32.0).astype(jnp.int32)
-                side = jnp.where(ratio >= looked_up(threshold, cell), cell + CELLS, cell)
-                value = ratio * looked_up(slope, side) + looked_up(intercept, side)
-                pair.append(value + dither_ref[here, over].astype(jnp.float32) * (1.0 / dither_steps))
-            held_ref[pl.ds(at, 16), part * LANES : (part + 1) * LANES] = jnp.concatenate(pair, axis=0).astype(jnp.bfloat16)
+            for row in range(0, deep, 16):
+                pair = jnp.concatenate([values[row, part], values[row + 8, part]], axis=0)
+                held_ref[over(row, part, 16)] = pair.astype(jnp.bfloat16)
         return carry
 
-    lax.fori_loop(0, blocks // 16, eight_rows, 0)
+    lax.fori_loop(0, blocks // deep, some_rows, 0)
     slotted = jnp.dot(order_ref[...], held_ref[...], preferred_element_type=jnp.float32)
-    symbols_ref[...] = slotted.astype(jnp.bfloat16)
+
+    def copy_out(which):
+        there = pl.ds(pl.multiple_of(which * columns, columns), columns)
+        slot = which % 2
+        return pltpu.make_async_copy(out_ref.at[slot], symbols_ref.at[:, there], out_sems.at[slot])
+
+    @pl.when(step >= 2)
+    def _():
+        copy_out(step - 2).wait()
+
+    out_ref[step % 2] = slotted.astype(jnp.bfloat16)
+    copy_out(step).start()
+
+    @pl.when(step == pl.num_programs(0) - 1)
+    def _():
+        copy_out(step - 1).wait()
+        copy_out(step).wait()
 
 
 def encode(rotated, dither, peaks, layout, levels):
     blocks, block = rotated.shape
-    columns = 512
+    columns = 1024
     return pl.pallas_call(
         encode_kernel,
         grid=(block // columns,),
@@ -204,60 +255,68 @@
             pl.BlockSpec((1, blocks), lambda i: (0, 0)),
         ],
         out_specs=[
-            pl.BlockSpec((blocks, columns), lambda i: (0, i)),
+            pl.BlockSpec(memory_space=pltpu.HBM),
             pl.BlockSpec((blocks, LANES), lambda i: (0, 0)),
         ],
         out_shape=[
-            jax.ShapeDtypeStruct((blocks, block), jnp.bfloat16),
+            pltpu.HBM((blocks, block), jnp.bfloat16),
             jax.ShapeDtypeStruct((blocks, LANES), jnp.float32),
         ],
         scratch_shapes=[
             pltpu.VMEM((blocks, LANES), jnp.float32),
             pltpu.VMEM((blocks, blocks), jnp.bfloat16),
             pltpu.VMEM((blocks, columns), jnp.bfloat16),
-        ],
-        compiler_params=pltpu.CompilerParams(vmem_limit_bytes=VMEM_BYTES),
+            pltpu.VMEM((3, 8, LANES), jnp.float32),
+            pltpu.VMEM((2 * levels.shape[0], 8, LANES), jnp.float32),
+            pltpu.VMEM((2, blocks, columns), jnp.bfloat16),
+            pltpu.SemaphoreType.DMA((2,)),
+        ],
+        compiler_params=pltpu.CompilerParams(vmem_limit_bytes=32 * MIB),
         name="encode",
     )(levels, rotated, dither, peaks, layout)
 
 
 def owner_kernel(
-    first_ref, levels_ref, symbols_ref, scales_ref, bits_ref, master_ref, moment_ref, second_ref,
+    place_ref, levels_ref, symbols_ref, scales_ref, bits_ref, master_ref, moment_ref, second_ref,
     new_master_ref, new_moment_ref, new_second_ref, copies_ref, total_ref, table_ref,
 ):
     step = pl.program_id(0)
     rows, block = total_ref.shape
+    replicas, _, columns = symbols_ref.shape
     count = levels_ref.shape[0]
-    slope, intercept = decode_tables(levels_ref)
 
     @pl.when(step == 0)
     def _():
-        total_ref[...] = jnp.zeros_like(total_ref)
         table = (hadamard(WIDE) * (1.0 / 64.0)).astype(jnp.bfloat16)
         for piece in range(3):
             table_ref[pl.ds(piece * WIDE, WIDE), :] = table
 
     def column(number, carry):
-        over = pl.ds(pl.multiple_of(number * LANES, LANES), LANES)
-        total = total_ref[:, over]
-        for replica in range(symbols_ref.shape[0]):
-            symbol = symbols_ref[replica, :, over].astype(jnp.float32)
-            symbol = jnp.minimum(jnp.maximum(symbol, 0.0), count - 1.0)
-            number_of = symbol.astype(jnp.int32)
-            total = total + (symbol * looked_up(slope, number_of) + looked_up(intercept, number_of))
-        total_ref[:, over] = total
+        here = pl.ds(pl.multiple_of(number * LANES, LANES), LANES)
+        there = pl.ds(pl.multiple_of(step * columns + number * LANES, LANES), LANES)
+        sums = [jnp.zeros((rows, LANES), jnp.float32) for _ in range(count)]
+        for replica in range(replicas):
+            symbol = symbols_ref[replica, :, here].astype(jnp.float32)
+            for level in range(count):
+                sums[level] = sums[level] + jnp.maximum(symbol, float(level))
+        total = jnp.full((rows, LANES), levels_ref[0] * float(replicas), jnp.float32)
+        for level in range(count - 1):
+            spacing = levels_ref[level + 1] - levels_ref[level]
+            total = total + spacing * ((sums[level] - sums[level + 1]) + float(replicas))
+        total_ref[:, there] = total
         return carry
 
-    lax.fori_loop(0, block // LANES, column, 0)
+    lax.fori_loop(0, columns // LANES, column, 0)
 
     @pl.when(step == pl.num_programs(0) - 1)
     def _():
         flips = (1 - 2 * bits_ref[...]).astype(jnp.float32)
         scales = jnp.concatenate([scales_ref[...]] * (WIDE // LANES), axis=1)
         parts = butterflies(total_ref[:, at : at + WIDE] * scales for at in range(0, block, WIDE))
-        for number, part in enumerate(parts):
+        turned = times_table(jnp.concatenate(parts, axis=0), table_ref[...])
+        for number in range(block // WIDE):
             over = slice(number * WIDE, (number + 1) * WIDE)
-            grads = times_table(part, table_ref[...]) * flips[:, over]
+            grads = turned[number * rows : (number + 1) * rows] * flips[:, over]
             moment = first_decay * moment_ref[:, over] + (1.0 - first_decay) * grads
             second = second_decay * second_ref[:, over] + (1.0 - second_decay) * grads * grads
             master = master_ref[:, over]
@@ -272,16 +331,16 @@
 
 def owner(place, levels, received, scales, bits, master, moment, second, copies):
     replicas, rows, block = received.shape
-    each = 8
+    columns = 1024
     whole = pl.BlockSpec((rows, block), lambda i, place: (0, 0))
     return pl.pallas_call(
         owner_kernel,
         grid_spec=pltpu.PrefetchScalarGridSpec(
             num_scalar_prefetch=1,
-            grid=(replicas // each,),
+            grid=(block // columns,),
             in_specs=[
                 pl.BlockSpec(memory_space=pltpu.SMEM),
-                pl.BlockSpec((each, rows, block), lambda i, place: (i, 0, 0)),
+                pl.BlockSpec((replicas, rows, columns), lambda i, place: (0, 0, i)),
                 pl.BlockSpec((rows, LANES), lambda i, place: (place[0], 0)),
                 pl.BlockSpec((1, block), lambda i, place: (0, 0)),
                 whole,

time: 135 us -> 99.4 us (0.74)
  Pallas kernels: 58.2 us -> 26 us
  local copies, waits for them, and re-layouts: 4.32 us -> 1.22 us
    pallas_call x1, Pallas kernels: 28.3 us -> 10.7 us  [encode(): pl.pallas_call(encode_kernel, grid=(block // columns,), in_specs=[pl.Bloc...]
    pallas_call x1, Pallas kernels: 16.7 us -> 7.16 us  [owner(): pl.pallas_call(owner_kernel, grid_spec=pltpu.PrefetchScalarGridSpec(num_s...]
    pallas_call x1, Pallas kernels: 10.5 us -> 5.58 us  [rotate(): pl.pallas_call(rotate_kernel, grid=(blocks // rows,), in_specs=[pl.BlockS...]
    unnamed x18 -> x16, local copies, waits for them, and re-layouts: 4 us -> 0.9 us
where the time goes in v2:
time: 99.4 us; the launch traced here: 99.1 us
  blocking collectives  34.7 us (35%)
  waiting for transfers between devices  30.3 us (30%)
  Pallas kernels  26 us (26%)
  starting transfers between devices  6.13 us (6%)
  local copies, waits for them, and re-layouts  1.22 us (1%)
    all_to_all x1, waiting for transfers between devices, local(): lax.all_to_all(symbols.reshape(groups, owned, block), axes, 0, 0, tiled=T...  28.4 us
    all_to_all x1, blocking collectives, local(): mine = lax.all_to_all(copies, chips, 0, 0, tiled=True)  18.6 us
    all_to_all x1, blocking collectives, local(): peaks = lax.all_to_all(peaks, axes, 0, 0, tiled=True)  16.1 us
    pallas_call x1, Pallas kernels, encode(): pl.pallas_call(encode_kernel, grid=(block // columns,), in_specs=[pl.Bloc...  10.7 us
    pallas_call x1, Pallas kernels, owner(): pl.pallas_call(owner_kernel, grid_spec=pltpu.PrefetchScalarGridSpec(num_s...  7.16 us
    pallas_call x1, Pallas kernels, rotate(): pl.pallas_call(rotate_kernel, grid=(blocks // rows,), in_specs=[pl.BlockS...  5.58 us
    all_to_all x1, starting transfers between devices, local(): lax.all_to_all(symbols.reshape(groups, owned, block), axes, 0, 0, tiled=T...  4.2 us
    pallas_call x1, Pallas kernels, reorder(): pl.pallas_call(reorder_kernel, grid=(block // columns,), in_specs=[pl.Blo...  2.64 us
  transfers between devices with their start and end apart: 2, of which 2 were waited for; matrix products, arithmetic and copies ran while one was open for 0% of the time, Pallas kernels for 0%

profile of v2, /device:TPU:1, one launch (start us, length us, event | category | flops | bytes accessed | tf_op | source)
XLA Modules:
  0.0 99.1 jit_solution(17937634737924964850)
XLA Ops:
  0.6 0.0 copy-start
  0.6 0.0 copy-start.4
  0.7 0.9 copy-done.4
  1.5 0.0 copy-start.6
  1.5 0.0 copy-start.7
  1.5 5.6 %rotate.1 = (f32[256,4096]{1,0:T(8,128)S(1)}, f32[32,8,128]{2,1,0:T(8,128)S(1)}) custom-call(f32[256,4096]{1,0:T(8,128)} %bitcast.24, s32[1,4096]{1,0:T(1,128)S(1)} %bitcast.21), custom_call_target="tpu_custom_call" | custom-call | tf_op jit(solution)/shard_map/rotate/pallas_call | solution.py:105
  7.1 16.1 %all_to_all.15.peaks_ref = f32[32,8,128]{2,1,0:T(8,128)S(1)} all-to-all(f32[32,8,128]{2,1,0:T(8,128)S(1)} %get-tuple-element.13), channel_id=1, replica_groups=mesh['section'=4,'dp_chip'=16,'dp_core'=2] {'dp_chip','dp_core'}, dimensions={0} | all-to-all | bytes 262144 | tf_op jit(solution)/shard_map/all_to_all | solution.py:397
  23.2 0.0 copy-done
  23.2 0.0 copy-done.6
  23.2 0.0 copy-done.7
  23.2 10.7 %encode.1 = (bf16[256,4096]{1,0:T(8,128)(2,1)}, f32[256,128]{1,0:T(8,128)S(1)}) custom-call(f32[16]{0:T(128)S(1)} %copy-done.7, f32[256,4096]{1,0:T(8,128)S(1)} %get-tuple-element.12.rotated_ref, s32[256,4096]{1,0:T(8,128)S(1)} %bitcast.16, f32[32,8,128]{2,1,0:T(8,128)S(1)} %all_to_all.15.peaks_ref, s32[1,256]{1,0:T(1,128)S(1)} %bitcast.23), custom_call_target="tpu_custom_call" | custom-call | tf_op jit(solution)/shard_map/encode/pallas_call | solution.py:247
  33.9 0.0 copy-start.1
  33.9 0.0 copy-start.2
  33.9 0.0 copy-start.3
  33.9 0.0 copy-start.5
  33.9 4.2 %all-to-all-start.1 = ((bf16[32,8,4096]{2,1,0:T(8,128)(2,1)}), bf16[32,8,4096]{2,1,0:T(8,128)(2,1)S(1)}, u32[]{:S(2)}, u32[]{:S(2)}) async-start(bf16[32,8,4096]{2,1,0:T(8,128)(2,1)} %bitcast.26), calls=%async_computation.1 | async-start | bytes 4194304 | tf_op jit(solution)/shard_map/all_to_all | solution.py:399
  38.1 28.4 %all-to-all-done.1.symbols_ref = bf16[32,8,4096]{2,1,0:T(8,128)(2,1)S(1)} async-done(((bf16[32,8,4096]{2,1,0:T(8,128)(2,1)}), bf16[32,8,4096]{2,1,0:T(8,128)(2,1)S(1)}, u32[]{:S(2)}, u32[]{:S(2)}) %all-to-all-start.1) | async-done | bytes 2097184 | tf_op jit(solution)/shard_map/all_to_all | solution.py:399
  66.5 0.0 copy-done.1
  66.5 0.0 copy-done.2
  66.5 0.0 copy-done.3
  66.5 0.0 copy-done.5
  66.5 7.2 %owner.1 = (f32[8,4096]{1,0:T(8,128)}, f32[8,4096]{1,0:T(8,128)}, f32[8,4096]{1,0:T(8,128)}, bf16[16,8,4096]{2,1,0:T(8,128)(2,1)S(1)}) custom-call(s32[1]{0:T(128)} %bitcast.place_ref, f32[16]{0:T(128)S(1)} %copy-done.7, bf16[32,8,4096]{2,1,0:T(8,128)(2,1)S(1)} %all-to-all-done.1.symbols_ref, f32[256,128]{1,0:T(8,128)S(1)} %get-tuple-element.15.scales_ref, ...), custom_call_target="tpu_custom_call" | custom-call | tf_op jit(solution)/shard_map/owner/pallas_call | solution.py:336
  73.7 18.6 %all_to_all.16 = bf16[16,8,4096]{2,1,0:T(8,128)(2,1)S(1)} all-to-all(bf16[16,8,4096]{2,1,0:T(8,128)(2,1)S(1)} %get-tuple-element.19), channel_id=1, replica_groups=mesh['section'=4,'dp_chip'=16,'dp_core'=2] {'dp_chip'}, dimensions={0} | all-to-all | bytes 2097152 | tf_op jit(solution)/shard_map/all_to_all | solution.py:404
  92.3 1.9 %collective-permute-start = (bf16[16,8,4096]{2,1,0:T(8,128)(2,1)S(1)}, bf16[16,8,4096]{2,1,0:T(8,128)(2,1)S(1)}, u32[]{:S(2)}, u32[]{:S(2)}) collective-permute-start(bf16[16,8,4096]{2,1,0:T(8,128)(2,1)S(1)} %all_to_all.16), channel_id=1, source_target_pairs={{0,1},{1,0},{2,3},{3,2},{4,5},{5,4},{6,7},{7,6},{8,9},{9,8},{10,11... | collective-permute-start | bytes 3145736 | tf_op jit(solution)/shard_map/ppermute | solution.py:405
  94.2 0.1 reshape.43
  94.3 0.1 dynamic-slice_reduce_fusion
  94.3 0.1 reshape.44.my_slots_ref
  94.4 0.1 reshape.45.other_slots_ref
  94.5 1.9 %collective-permute-done = bf16[16,8,4096]{2,1,0:T(8,128)(2,1)S(1)} collective-permute-done((bf16[16,8,4096]{2,1,0:T(8,128)(2,1)S(1)}, bf16[16,8,4096]{2,1,0:T(8,128)(2,1)S(1)}, u32[]{:S(2)}, u32[]{:S(2)}) %collective-permute-start) | collective-permute-done | bytes 1048608 | tf_op jit(solution)/shard_map/ppermute | solution.py:405
  96.5 2.6 %reorder.1 = bf16[256,4096]{1,0:T(8,128)(2,1)} custom-call(bf16[128,4096]{1,0:T(8,128)(2,1)S(1)} %bitcast.15, bf16[128,4096]{1,0:T(8,128)(2,1)S(1)} %bitcast.17, s32[1,128]{1,0:T(1,128)S(1)} %reshape.44.my_slots_ref, s32[1,128]{1,0:T(1,128)S(1)} %reshape.45.other_slots_ref), custom_call_target="tpu_custom_call" | custom-call | tf_op jit(solution)/shard_map/reorder/pallas_call | solution.py:374
Async XLA Ops:
  0.6 22.6 %copy-start = (s32[1,1,256,4096]{3,2,1,0:T(8,128)S(1)}, s32[1,1,256,4096]{3,2,1,0:T(8,128)}, u32[]{:S(2)}) copy-start(s32[1,1,256,4096]{3,2,1,0:T(8,128)} %param.9) | copy-start | bytes 12582916
  0.6 0.9 copy-start.4
  1.5 21.7 %copy-start.6 = (s32[256]{0:T(256)S(1)}, s32[256]{0:T(256)}, u32[]{:S(2)}) copy-start(s32[256]{0:T(256)} %param.12) | copy-start | bytes 3076
  1.5 21.7 %copy-start.7 = (f32[16]{0:T(128)S(1)}, f32[16]{0:T(128)}, u32[]{:S(2)}) copy-start(f32[16]{0:T(128)} %levels_ref.3) | copy-start | bytes 196
  33.9 32.6 %copy-start.1 = (f32[1,8,4096]{2,1,0:T(8,128)S(1)}, f32[1,8,4096]{2,1,0:T(8,128)}, u32[]{:S(2)}) copy-start(f32[1,8,4096]{2,1,0:T(8,128)} %param.13) | copy-start | bytes 393220
  33.9 32.6 %copy-start.2 = (f32[1,8,4096]{2,1,0:T(8,128)S(1)}, f32[1,8,4096]{2,1,0:T(8,128)}, u32[]{:S(2)}) copy-start(f32[1,8,4096]{2,1,0:T(8,128)} %param.14) | copy-start | bytes 393220
  33.9 32.6 %copy-start.3 = (f32[1,8,4096]{2,1,0:T(8,128)S(1)}, f32[1,8,4096]{2,1,0:T(8,128)}, u32[]{:S(2)}) copy-start(f32[1,8,4096]{2,1,0:T(8,128)} %param.15) | copy-start | bytes 393220
  33.9 32.6 %copy-start.5 = (s32[4096]{0:T(1024)S(1)}, s32[4096]{0:T(1024)}, u32[]{:S(2)}) copy-start(s32[4096]{0:T(1024)} %param.10) | copy-start | bytes 49156
  33.9 32.6 %all-to-all-start.1 = ((bf16[32,8,4096]{2,1,0:T(8,128)(2,1)}), bf16[32,8,4096]{2,1,0:T(8,128)(2,1)S(1)}, u32[]{:S(2)}, u32[]{:S(2)}) async-start(bf16[32,8,4096]{2,1,0:T(8,128)(2,1)} %bitcast.26), calls=%async_computation.1 | async-start | bytes 4194304 | tf_op jit(solution)/shard_map/all_to_all | solution.py:399
  92.3 4.2 %collective-permute-start = (bf16[16,8,4096]{2,1,0:T(8,128)(2,1)S(1)}, bf16[16,8,4096]{2,1,0:T(8,128)(2,1)S(1)}, u32[]{:S(2)}, u32[]{:S(2)}) collective-permute-start(bf16[16,8,4096]{2,1,0:T(8,128)(2,1)S(1)} %all_to_all.16), channel_id=1, source_target_pairs={{0,1},{1,0},{2,3},{3,2},{4,5},{5,4},{6,7},{7,6},{8,9},{9,8},{10,11... | collective-permute-start | bytes 3145736 | tf_op jit(solution)/shard_map/ppermute | solution.py:405

commit v3 on v2

--- a/solution.py
+++ b/solution.py
@@ -161,7 +161,8 @@
     inverse_ref, order_ref, held_ref, tables_ref, lines_ref, out_ref, out_sems,
 ):
     step = pl.program_id(0)
-    blocks, columns = rotated_ref.shape
+    blocks = rotated_ref.shape[0]
+    columns = held_ref.shape[1]
     count = levels_ref.shape[0]
 
     @pl.when(step == 0)
@@ -183,7 +184,7 @@
             lines_ref[2 * number + 1] = intercept
 
     threshold, slope, intercept = tables_ref[0], tables_ref[1], tables_ref[2]
-    deep = 64
+    deep = 128
 
     def some_rows(number, carry):
         start = pl.multiple_of(number * deep, deep)
@@ -192,7 +193,10 @@
         def over(row, part, height=8):
             return pl.ds(pl.multiple_of(start + row, height), height), slice(part * LANES, (part + 1) * LANES)
 
-        ratios = {tile: rotated_ref[over(*tile)] * inverse_ref[over(tile[0], 0)] for tile in tiles}
+        def whole(row, part):
+            return pl.ds(pl.multiple_of(start + row, 8), 8), pl.ds(pl.multiple_of(step * columns + part * LANES, LANES), LANES)
+
+        ratios = {tile: rotated_ref[whole(*tile)] * inverse_ref[over(tile[0], 0)] for tile in tiles}
         by_table = tiles[1::2]
         cells = {tile: (ratios[tile] * CELL_RATE + 32.0).astype(jnp.int32) for tile in by_table}
         limits = {tile: looked_up(threshold, cells[tile]) for tile in by_table}
@@ -213,7 +217,7 @@
                     its_slope = jnp.where(above, lines_ref[2 * level], its_slope)
                     its_intercept = jnp.where(above, lines_ref[2 * level + 1], its_intercept)
                 value = ratio * its_slope + its_intercept
-            values[tile] = value + dither_ref[over(*tile)].astype(jnp.float32) * (1.0 / dither_steps)
+            values[tile] = value + dither_ref[whole(*tile)].astype(jnp.float32) * (1.0 / dither_steps)
         for part in range(columns // LANES):
             for row in range(0, deep, 16):
                 pair = jnp.concatenate([values[row, part], values[row + 8, part]], axis=0)
@@ -249,8 +253,8 @@
         grid=(block // columns,),
         in_specs=[
             pl.BlockSpec(memory_space=pltpu.SMEM),
-            pl.BlockSpec((blocks, columns), lambda i: (0, i)),
-            pl.BlockSpec((blocks, columns), lambda i: (0, i)),
+            pl.BlockSpec(memory_space=pltpu.VMEM),
+            pl.BlockSpec(memory_space=pltpu.VMEM),
             pl.BlockSpec(peaks.shape, lambda i: (0, 0, 0)),
             pl.BlockSpec((1, blocks), lambda i: (0, 0)),
         ],
@@ -282,7 +286,8 @@
 ):
     step = pl.program_id(0)
     rows, block = total_ref.shape
-    replicas, _, columns = symbols_ref.shape
+    replicas = symbols_ref.shape[0]
+    columns = block // pl.num_programs(0)
     count = levels_ref.shape[0]
 
     @pl.when(step == 0)
@@ -292,11 +297,10 @@
             table_ref[pl.ds(piece * WIDE, WIDE), :] = table
 
     def column(number, carry):
-        here = pl.ds(pl.multiple_of(number * LANES, LANES), LANES)
         there = pl.ds(pl.multiple_of(step * columns + number * LANES, LANES), LANES)
         sums = [jnp.zeros((rows, LANES), jnp.float32) for _ in range(count)]
         for replica in range(replicas):
-            symbol = symbols_ref[replica, :, here].astype(jnp.float32)
+            symbol = symbols_ref[replica, :, there].astype(jnp.float32)
             for level in range(count):
                 sums[level] = sums[level] + jnp.maximum(symbol, float(level))
         total = jnp.full((rows, LANES), levels_ref[0] * float(replicas), jnp.float32)
@@ -331,7 +335,7 @@
 
 def owner(place, levels, received, scales, bits, master, moment, second, copies):
     replicas, rows, block = received.shape
-    columns = 1024
+    columns = block
     whole = pl.BlockSpec((rows, block), lambda i, place: (0, 0))
     return pl.pallas_call(
         owner_kernel,
@@ -340,7 +344,7 @@
             grid=(block // columns,),
             in_specs=[
                 pl.BlockSpec(memory_space=pltpu.SMEM),
-                pl.BlockSpec((replicas, rows, columns), lambda i, place: (0, 0, i)),
+                pl.BlockSpec(memory_space=pltpu.VMEM),
                 pl.BlockSpec((rows, LANES), lambda i, place: (place[0], 0)),
                 pl.BlockSpec((1, block), lambda i, place: (0, 0)),
                 whole,
@@ -364,7 +368,8 @@
     my_order = (row == my_slots_ref[...]).astype(jnp.float32).astype(jnp.bfloat16)
     other_order = (row == other_slots_ref[...]).astype(jnp.float32).astype(jnp.bfloat16)
     order = jnp.concatenate([my_order, other_order], axis=1)
-    held = jnp.concatenate([mine_ref[...], others_ref[...]], axis=0)
+    here = pl.ds(pl.multiple_of(pl.program_id(0) * out_ref.shape[1], LANES), out_ref.shape[1])
+    held = jnp.concatenate([mine_ref[:, here], others_ref[:, here]], axis=0)
     out_ref[...] = jnp.dot(order, held, preferred_element_type=jnp.float32).astype(jnp.bfloat16)
 
 
@@ -375,8 +380,8 @@
         reorder_kernel,
         grid=(block // columns,),
         in_specs=[
-            pl.BlockSpec((half, columns), lambda i: (0, i)),
-            pl.BlockSpec((half, columns), lambda i: (0, i)),
+            pl.BlockSpec(memory_space=pltpu.VMEM),
+            pl.BlockSpec(memory_space=pltpu.VMEM),
             pl.BlockSpec((1, half), lambda i: (0, 0)),
             pl.BlockSpec((1, half), lambda i: (0, 0)),
         ],
@@ -393,7 +398,8 @@
     blocks, block = gradient.shape[2:]
     owned = blocks // groups
     bits = sign_bits.reshape(1, block)
-    rotated, peaks = rotate(gradient[0, 0], bits, groups)
+    rotated, peaks = rotate(gradient[0, 0], pltpu.with_memory_space_constraint(bits, pltpu.HBM), groups)
+    dither, rotated, peaks = lax.optimization_barrier((dither, rotated, peaks))
     peaks = lax.all_to_all(peaks, axes, 0, 0, tiled=True)
     symbols, scales = encode(rotated, dither[0, 0], peaks, layout.reshape(1, blocks), levels)
     received = lax.all_to_all(symbols.reshape(groups, owned, block), axes, 0, 0, tiled=True)

time: 99.4 us -> 96.2 us (0.968)
  Pallas kernels: 26 us -> 23.7 us
    pallas_call x1, Pallas kernels: 10.7 us -> 8.94 us  [encode(): pl.pallas_call(encode_kernel, grid=(block // columns,), in_specs=[pl.Bloc...]
where the time goes in v3:
time: 96.2 us; the launch traced here: 95.9 us
  blocking collectives  34.7 us (36%)
  waiting for transfers between devices  30.3 us (31%)
  Pallas kernels  23.7 us (25%)
  starting transfers between devices  6.13 us (6%)
    all_to_all x1, waiting for transfers between devices, local(): lax.all_to_all(symbols.reshape(groups, owned, block), axes, 0, 0, tiled=T...  28.4 us
    all_to_all x1, blocking collectives, local(): mine = lax.all_to_all(copies, chips, 0, 0, tiled=True)  18.6 us
    all_to_all x1, blocking collectives, local(): peaks = lax.all_to_all(peaks, axes, 0, 0, tiled=True)  16.1 us
    pallas_call x1, Pallas kernels, encode(): pl.pallas_call(encode_kernel, grid=(block // columns,), in_specs=[pl.Bloc...  8.94 us
    pallas_call x1, Pallas kernels, owner(): pl.pallas_call(owner_kernel, grid_spec=pltpu.PrefetchScalarGridSpec(num_s...  6.89 us
    pallas_call x1, Pallas kernels, rotate(): pl.pallas_call(rotate_kernel, grid=(blocks // rows,), in_specs=[pl.BlockS...  5.32 us
    all_to_all x1, starting transfers between devices, local(): lax.all_to_all(symbols.reshape(groups, owned, block), axes, 0, 0, tiled=T...  4.21 us
    pallas_call x1, Pallas kernels, reorder(): pl.pallas_call(reorder_kernel, grid=(block // columns,), in_specs=[pl.Blo...  2.51 us
  transfers between devices with their start and end apart: 2, of which 2 were waited for; matrix products, arithmetic and copies ran while one was open for 0% of the time, Pallas kernels for 0%

profile of v3, /device:TPU:1, one launch (start us, length us, event | category | flops | bytes accessed | tf_op | source)
XLA Modules:
  0.0 95.9 jit_solution(12184884468252282207)
XLA Ops:
  0.6 0.0 copy-start
  0.6 0.0 copy-start.5
  0.7 0.0 copy-start.6
  0.7 5.3 %rotate.1 = (f32[256,4096]{1,0:T(8,128)S(1)}, f32[32,8,128]{2,1,0:T(8,128)S(1)}) custom-call(f32[256,4096]{1,0:T(8,128)} %bitcast.24, s32[1,4096]{1,0:T(1,128)} %bitcast.21), custom_call_target="tpu_custom_call" | custom-call | tf_op jit(solution)/shard_map/rotate/pallas_call | solution.py:105
  6.0 16.1 %all_to_all.15.peaks_ref = f32[32,8,128]{2,1,0:T(8,128)S(1)} all-to-all(f32[32,8,128]{2,1,0:T(8,128)S(1)} %get-tuple-element.19), channel_id=1, replica_groups=mesh['section'=4,'dp_chip'=16,'dp_core'=2] {'dp_chip','dp_core'}, dimensions={0} | all-to-all | bytes 262144 | tf_op jit(solution)/shard_map/all_to_all | solution.py:403
  22.1 0.0 copy-done
  22.1 0.0 copy-done.5
  22.1 0.0 copy-done.6
  22.1 8.9 %encode.1 = (bf16[256,4096]{1,0:T(8,128)(2,1)}, f32[256,128]{1,0:T(8,128)S(1)}) custom-call(f32[16]{0:T(128)S(1)} %copy-done.6, f32[256,4096]{1,0:T(8,128)S(1)} %get-tuple-element.17.rotated_ref, s32[256,4096]{1,0:T(8,128)S(1)} %bitcast.16, f32[32,8,128]{2,1,0:T(8,128)S(1)} %all_to_all.15.peaks_ref, s32[1,256]{1,0:T(1,128)S(1)} %bitcast.23), custom_call_target="tpu_custom_call" | custom-call | tf_op jit(solution)/shard_map/encode/pallas_call | solution.py:251
  31.0 0.0 copy-start.1
  31.1 0.0 copy-start.2
  31.1 0.0 copy-start.3
  31.1 0.0 copy-start.4
  31.1 4.2 %all-to-all-start.1 = ((bf16[32,8,4096]{2,1,0:T(8,128)(2,1)}), bf16[32,8,4096]{2,1,0:T(8,128)(2,1)S(1)}, u32[]{:S(2)}, u32[]{:S(2)}) async-start(bf16[32,8,4096]{2,1,0:T(8,128)(2,1)} %bitcast.26), calls=%async_computation.1 | async-start | bytes 4194304 | tf_op jit(solution)/shard_map/all_to_all | solution.py:405
  35.3 28.4 %all-to-all-done.1.symbols_ref = bf16[32,8,4096]{2,1,0:T(8,128)(2,1)S(1)} async-done(((bf16[32,8,4096]{2,1,0:T(8,128)(2,1)}), bf16[32,8,4096]{2,1,0:T(8,128)(2,1)S(1)}, u32[]{:S(2)}, u32[]{:S(2)}) %all-to-all-start.1) | async-done | bytes 2097184 | tf_op jit(solution)/shard_map/all_to_all | solution.py:405
  63.7 0.0 copy-done.1
  63.7 0.0 copy-done.2
  63.7 0.0 copy-done.3
  63.7 0.0 copy-done.4
  63.7 6.9 %owner.1 = (f32[8,4096]{1,0:T(8,128)}, f32[8,4096]{1,0:T(8,128)}, f32[8,4096]{1,0:T(8,128)}, bf16[16,8,4096]{2,1,0:T(8,128)(2,1)S(1)}) custom-call(s32[1]{0:T(128)} %bitcast.place_ref, f32[16]{0:T(128)S(1)} %copy-done.6, bf16[32,8,4096]{2,1,0:T(8,128)(2,1)S(1)} %all-to-all-done.1.symbols_ref, f32[256,128]{1,0:T(8,128)S(1)} %get-tuple-element.21.scales_ref, ...), custom_call_target="tpu_custom_call" | custom-call | tf_op jit(solution)/shard_map/owner/pallas_call | solution.py:340
  70.6 18.6 %all_to_all.16 = bf16[16,8,4096]{2,1,0:T(8,128)(2,1)S(1)} all-to-all(bf16[16,8,4096]{2,1,0:T(8,128)(2,1)S(1)} %get-tuple-element.25), channel_id=1, replica_groups=mesh['section'=4,'dp_chip'=16,'dp_core'=2] {'dp_chip'}, dimensions={0} | all-to-all | bytes 2097152 | tf_op jit(solution)/shard_map/all_to_all | solution.py:410
  89.2 1.9 %collective-permute-start = (bf16[16,8,4096]{2,1,0:T(8,128)(2,1)S(1)}, bf16[16,8,4096]{2,1,0:T(8,128)(2,1)S(1)}, u32[]{:S(2)}, u32[]{:S(2)}) collective-permute-start(bf16[16,8,4096]{2,1,0:T(8,128)(2,1)S(1)} %all_to_all.16), channel_id=1, source_target_pairs={{0,1},{1,0},{2,3},{3,2},{4,5},{5,4},{6,7},{7,6},{8,9},{9,8},{10,11... | collective-permute-start | bytes 3145736 | tf_op jit(solution)/shard_map/ppermute | solution.py:411
  91.1 0.1 reshape.43
  91.2 0.1 dynamic-slice_reduce_fusion
  91.3 0.1 reshape.44.my_slots_ref
  91.3 0.1 reshape.45.other_slots_ref
  91.4 1.9 %collective-permute-done = bf16[16,8,4096]{2,1,0:T(8,128)(2,1)S(1)} collective-permute-done((bf16[16,8,4096]{2,1,0:T(8,128)(2,1)S(1)}, bf16[16,8,4096]{2,1,0:T(8,128)(2,1)S(1)}, u32[]{:S(2)}, u32[]{:S(2)}) %collective-permute-start) | collective-permute-done | bytes 1048608 | tf_op jit(solution)/shard_map/ppermute | solution.py:411
  93.4 2.5 %reorder.1 = bf16[256,4096]{1,0:T(8,128)(2,1)} custom-call(bf16[128,4096]{1,0:T(8,128)(2,1)S(1)} %bitcast.15, bf16[128,4096]{1,0:T(8,128)(2,1)S(1)} %bitcast.17, s32[1,128]{1,0:T(1,128)S(1)} %reshape.44.my_slots_ref, s32[1,128]{1,0:T(1,128)S(1)} %reshape.45.other_slots_ref), custom_call_target="tpu_custom_call" | custom-call | tf_op jit(solution)/shard_map/reorder/pallas_call | solution.py:379
Async XLA Ops:
  0.6 21.5 %copy-start = (s32[1,1,256,4096]{3,2,1,0:T(8,128)S(1)}, s32[1,1,256,4096]{3,2,1,0:T(8,128)}, u32[]{:S(2)}) copy-start(s32[1,1,256,4096]{3,2,1,0:T(8,128)} %param.9) | copy-start | bytes 12582916
  0.6 21.4 %copy-start.5 = (s32[256]{0:T(256)S(1)}, s32[256]{0:T(256)}, u32[]{:S(2)}) copy-start(s32[256]{0:T(256)} %param.12) | copy-start | bytes 3076
  0.7 21.4 %copy-start.6 = (f32[16]{0:T(128)S(1)}, f32[16]{0:T(128)}, u32[]{:S(2)}) copy-start(f32[16]{0:T(128)} %levels_ref.3) | copy-start | bytes 196
  31.0 32.6 %copy-start.1 = (f32[1,8,4096]{2,1,0:T(8,128)S(1)}, f32[1,8,4096]{2,1,0:T(8,128)}, u32[]{:S(2)}) copy-start(f32[1,8,4096]{2,1,0:T(8,128)} %param.13) | copy-start | bytes 393220
  31.1 32.6 %copy-start.2 = (f32[1,8,4096]{2,1,0:T(8,128)S(1)}, f32[1,8,4096]{2,1,0:T(8,128)}, u32[]{:S(2)}) copy-start(f32[1,8,4096]{2,1,0:T(8,128)} %param.14) | copy-start | bytes 393220
  31.1 32.6 %copy-start.3 = (f32[1,8,4096]{2,1,0:T(8,128)S(1)}, f32[1,8,4096]{2,1,0:T(8,128)}, u32[]{:S(2)}) copy-start(f32[1,8,4096]{2,1,0:T(8,128)} %param.15) | copy-start | bytes 393220
  31.1 32.6 %copy-start.4 = (s32[4096]{0:T(1024)S(1)}, s32[4096]{0:T(1024)}, u32[]{:S(2)}) copy-start(s32[4096]{0:T(1024)} %param.10) | copy-start | bytes 49156
  31.1 32.6 %all-to-all-start.1 = ((bf16[32,8,4096]{2,1,0:T(8,128)(2,1)}), bf16[32,8,4096]{2,1,0:T(8,128)(2,1)S(1)}, u32[]{:S(2)}, u32[]{:S(2)}) async-start(bf16[32,8,4096]{2,1,0:T(8,128)(2,1)} %bitcast.26), calls=%async_computation.1 | async-start | bytes 4194304 | tf_op jit(solution)/shard_map/all_to_all | solution.py:405
  89.2 4.2 %collective-permute-start = (bf16[16,8,4096]{2,1,0:T(8,128)(2,1)S(1)}, bf16[16,8,4096]{2,1,0:T(8,128)(2,1)S(1)}, u32[]{:S(2)}, u32[]{:S(2)}) collective-permute-start(bf16[16,8,4096]{2,1,0:T(8,128)(2,1)S(1)} %all_to_all.16), channel_id=1, source_target_pairs={{0,1},{1,0},{2,3},{3,2},{4,5},{5,4},{6,7},{7,6},{8,9},{9,8},{10,11... | collective-permute-start | bytes 3145736 | tf_op jit(solution)/shard_map/ppermute | solution.py:411

commit v4 on v3

--- a/solution.py
+++ b/solution.py
@@ -157,8 +157,8 @@
 
 
 def encode_kernel(
-    levels_ref, rotated_ref, dither_ref, peaks_ref, layout_ref, symbols_ref, scales_ref,
-    inverse_ref, order_ref, held_ref, tables_ref, lines_ref, out_ref, out_sems,
+    core, levels_ref, rotated_ref, dither_ref, peaks_ref, layout_ref, mine_ref, others_ref, scales_ref,
+    inverse_ref, order_ref, held_ref, tables_ref, lines_ref,
 ):
     step = pl.program_id(0)
     blocks = rotated_ref.shape[0]
@@ -171,7 +171,11 @@
         wide = jnp.concatenate([lines[i : i + 1, :] for i in range(blocks // LANES)], axis=1)
         order = lax.broadcasted_iota(jnp.int32, (blocks, blocks), 0) == layout_ref[...]
         order = jnp.transpose(order.astype(jnp.float32))
-        order_ref[...] = order.astype(jnp.bfloat16)
+        by_core = order.reshape(blocks // 16, 2, 8, blocks)
+        first, second = by_core[:, 0].reshape(blocks // 2, blocks), by_core[:, 1].reshape(blocks // 2, blocks)
+        is_first = lax.axis_index(core) == 0
+        grouped = [jnp.where(is_first, first, second), jnp.where(is_first, second, first)]
+        order_ref[...] = jnp.concatenate(grouped, axis=0).astype(jnp.bfloat16)
         slot = jnp.sum(jnp.where(order > 0.5, wide, 0.0), axis=1, keepdims=True)
         scales_ref[...] = jnp.broadcast_to(slot, (blocks, LANES))
         for at in range(blocks // LANES):
@@ -227,29 +231,16 @@
     lax.fori_loop(0, blocks // deep, some_rows, 0)
     slotted = jnp.dot(order_ref[...], held_ref[...], preferred_element_type=jnp.float32)
 
-    def copy_out(which):
-        there = pl.ds(pl.multiple_of(which * columns, columns), columns)
-        slot = which % 2
-        return pltpu.make_async_copy(out_ref.at[slot], symbols_ref.at[:, there], out_sems.at[slot])
-
-    @pl.when(step >= 2)
-    def _():
-        copy_out(step - 2).wait()
-
-    out_ref[step % 2] = slotted.astype(jnp.bfloat16)
-    copy_out(step).start()
-
-    @pl.when(step == pl.num_programs(0) - 1)
-    def _():
-        copy_out(step - 1).wait()
-        copy_out(step).wait()
-
-
-def encode(rotated, dither, peaks, layout, levels):
+    there = pl.ds(pl.multiple_of(step * columns, columns), columns)
+    mine_ref[:, there] = slotted[: blocks // 2].astype(jnp.bfloat16)
+    others_ref[:, there] = slotted[blocks // 2 :].astype(jnp.bfloat16)
+
+
+def encode(core, rotated, dither, peaks, layout, levels):
     blocks, block = rotated.shape
     columns = 1024
     return pl.pallas_call(
-        encode_kernel,
+        functools.partial(encode_kernel, core),
         grid=(block // columns,),
         in_specs=[
             pl.BlockSpec(memory_space=pltpu.SMEM),
@@ -259,11 +250,13 @@
             pl.BlockSpec((1, blocks), lambda i: (0, 0)),
         ],
         out_specs=[
-            pl.BlockSpec(memory_space=pltpu.HBM),
+            pl.BlockSpec(memory_space=pltpu.VMEM),
+            pl.BlockSpec(memory_space=pltpu.VMEM),
             pl.BlockSpec((blocks, LANES), lambda i: (0, 0)),
         ],
         out_shape=[
-            pltpu.HBM((blocks, block), jnp.bfloat16),
+            pltpu.VMEM((blocks // 2, block), jnp.bfloat16),
+            pltpu.VMEM((blocks // 2, block), jnp.bfloat16),
             jax.ShapeDtypeStruct((blocks, LANES), jnp.float32),
         ],
         scratch_shapes=[
@@ -272,79 +265,83 @@
             pltpu.VMEM((blocks, columns), jnp.bfloat16),
             pltpu.VMEM((3, 8, LANES), jnp.float32),
             pltpu.VMEM((2 * levels.shape[0], 8, LANES), jnp.float32),
-            pltpu.VMEM((2, blocks, columns), jnp.bfloat16),
-            pltpu.SemaphoreType.DMA((2,)),
         ],
         compiler_params=pltpu.CompilerParams(vmem_limit_bytes=32 * MIB),
         name="encode",
     )(levels, rotated, dither, peaks, layout)
 
 
+def merge_kernel(levels_ref, mine_ref, theirs_ref, out_ref):
+    count = levels_ref.shape[0]
+    rows, block = out_ref.shape
+    wide = 1024
+    spacings = [levels_ref[level + 1] - levels_ref[level] for level in range(count - 1)]
+    weights = [spacings[0]] + [spacings[level] - spacings[level - 1] for level in range(1, count - 1)] + [-spacings[-1]]
+
+    def some(number, carry):
+        here = pl.ds(pl.multiple_of(number // (block // wide) * 16, 16), 16)
+        start = number % (block // wide) * wide
+        for part in range(wide // LANES):
+            there = pl.ds(pl.multiple_of(start + part * LANES, LANES), LANES)
+            one, two = mine_ref[here, there].astype(jnp.float32), theirs_ref[here, there].astype(jnp.float32)
+            total = jnp.full((16, LANES), 2.0 * levels_ref[count - 1], jnp.float32)
+            for level in range(count):
+                total = total + weights[level] * (jnp.maximum(one, float(level)) + jnp.maximum(two, float(level)))
+            out_ref[here, there] = total
+        return carry
+
+    lax.fori_loop(0, rows // 16 * (block // wide), some, 0)
+
+
+def merge(levels, mine, theirs):
+    here = pl.BlockSpec(memory_space=pltpu.VMEM)
+    return pl.pallas_call(
+        merge_kernel,
+        in_specs=[pl.BlockSpec(memory_space=pltpu.SMEM), here, here],
+        out_specs=here,
+        out_shape=pltpu.VMEM(mine.shape, jnp.float32),
+        compiler_params=pltpu.CompilerParams(vmem_limit_bytes=VMEM_BYTES),
+        name="merge",
+    )(levels, mine, theirs)
+
+
 def owner_kernel(
-    place_ref, levels_ref, symbols_ref, scales_ref, bits_ref, master_ref, moment_ref, second_ref,
-    new_master_ref, new_moment_ref, new_second_ref, copies_ref, total_ref, table_ref,
+    place_ref, total_ref, scales_ref, bits_ref, master_ref, moment_ref, second_ref,
+    new_master_ref, new_moment_ref, new_second_ref, copies_ref, table_ref,
 ):
-    step = pl.program_id(0)
     rows, block = total_ref.shape
-    replicas = symbols_ref.shape[0]
-    columns = block // pl.num_programs(0)
-    count = levels_ref.shape[0]
-
-    @pl.when(step == 0)
-    def _():
-        table = (hadamard(WIDE) * (1.0 / 64.0)).astype(jnp.bfloat16)
-        for piece in range(3):
-            table_ref[pl.ds(piece * WIDE, WIDE), :] = table
-
-    def column(number, carry):
-        there = pl.ds(pl.multiple_of(step * columns + number * LANES, LANES), LANES)
-        sums = [jnp.zeros((rows, LANES), jnp.float32) for _ in range(count)]
-        for replica in range(replicas):
-            symbol = symbols_ref[replica, :, there].astype(jnp.float32)
-            for level in range(count):
-                sums[level] = sums[level] + jnp.maximum(symbol, float(level))
-        total = jnp.full((rows, LANES), levels_ref[0] * float(replicas), jnp.float32)
-        for level in range(count - 1):
-            spacing = levels_ref[level + 1] - levels_ref[level]
-            total = total + spacing * ((sums[level] - sums[level + 1]) + float(replicas))
-        total_ref[:, there] = total
-        return carry
-
-    lax.fori_loop(0, columns // LANES, column, 0)
-
-    @pl.when(step == pl.num_programs(0) - 1)
-    def _():
-        flips = (1 - 2 * bits_ref[...]).astype(jnp.float32)
-        scales = jnp.concatenate([scales_ref[...]] * (WIDE // LANES), axis=1)
-        parts = butterflies(total_ref[:, at : at + WIDE] * scales for at in range(0, block, WIDE))
-        turned = times_table(jnp.concatenate(parts, axis=0), table_ref[...])
-        for number in range(block // WIDE):
-            over = slice(number * WIDE, (number + 1) * WIDE)
-            grads = turned[number * rows : (number + 1) * rows] * flips[:, over]
-            moment = first_decay * moment_ref[:, over] + (1.0 - first_decay) * grads
-            second = second_decay * second_ref[:, over] + (1.0 - second_decay) * grads * grads
-            master = master_ref[:, over]
-            updated = master - learning_rate * (moment / (jnp.sqrt(second) + adam_epsilon) + weight_decay * master)
-            new_moment_ref[:, over] = moment
-            new_second_ref[:, over] = second
-            new_master_ref[:, over] = updated
-            rounded = updated.astype(jnp.bfloat16)
-            for copy in range(copies_ref.shape[0]):
-                copies_ref[copy, :, over] = rounded
-
-
-def owner(place, levels, received, scales, bits, master, moment, second, copies):
-    replicas, rows, block = received.shape
-    columns = block
+    table = (hadamard(WIDE) * (1.0 / 64.0)).astype(jnp.bfloat16)
+    for piece in range(3):
+        table_ref[pl.ds(piece * WIDE, WIDE), :] = table
+    flips = (1 - 2 * bits_ref[...]).astype(jnp.float32)
+    scales = jnp.concatenate([scales_ref[...]] * (WIDE // LANES), axis=1)
+    parts = butterflies(total_ref[:, at : at + WIDE] * scales for at in range(0, block, WIDE))
+    turned = times_table(jnp.concatenate(parts, axis=0), table_ref[...])
+    for number in range(block // WIDE):
+        over = slice(number * WIDE, (number + 1) * WIDE)
+        grads = turned[number * rows : (number + 1) * rows] * flips[:, over]
+        moment = first_decay * moment_ref[:, over] + (1.0 - first_decay) * grads
+        second = second_decay * second_ref[:, over] + (1.0 - second_decay) * grads * grads
+        master = master_ref[:, over]
+        updated = master - learning_rate * (moment / (jnp.sqrt(second) + adam_epsilon) + weight_decay * master)
+        new_moment_ref[:, over] = moment
+        new_second_ref[:, over] = second
+        new_master_ref[:, over] = updated
+        rounded = updated.astype(jnp.bfloat16)
+        for copy in range(copies_ref.shape[0]):
+            copies_ref[copy, :, over] = rounded
+
+
+def owner(place, total, scales, bits, master, moment, second, copies):
+    rows, block = total.shape
     whole = pl.BlockSpec((rows, block), lambda i, place: (0, 0))
     return pl.pallas_call(
         owner_kernel,
         grid_spec=pltpu.PrefetchScalarGridSpec(
             num_scalar_prefetch=1,
-            grid=(block // columns,),
+            grid=(1,),
             in_specs=[
-                pl.BlockSpec(memory_space=pltpu.SMEM),
-                pl.BlockSpec(memory_space=pltpu.VMEM),
+                whole,
                 pl.BlockSpec((rows, LANES), lambda i, place: (place[0], 0)),
                 pl.BlockSpec((1, block), lambda i, place: (0, 0)),
                 whole,
@@ -352,13 +349,13 @@
                 whole,
             ],
             out_specs=[whole, whole, whole, pl.BlockSpec((copies, rows, block), lambda i, place: (0, 0, 0))],
-            scratch_shapes=[pltpu.VMEM((rows, block), jnp.float32), pltpu.VMEM((3 * WIDE, WIDE), jnp.bfloat16)],
+            scratch_shapes=[pltpu.VMEM((3 * WIDE, WIDE), jnp.bfloat16)],
         ),
         out_shape=[jax.ShapeDtypeStruct((rows, block), jnp.float32)] * 3
         + [jax.ShapeDtypeStruct((copies, rows, block), jnp.bfloat16)],
         compiler_params=pltpu.CompilerParams(vmem_limit_bytes=VMEM_BYTES),
         name="owner",
-    )(place, levels, received, scales, bits, master, moment, second)
+    )(place, total, scales, bits, master, moment, second)
 
 
 def reorder_kernel(mine_ref, others_ref, my_slots_ref, other_slots_ref, out_ref):
@@ -401,11 +398,14 @@
     rotated, peaks = rotate(gradient[0, 0], pltpu.with_memory_space_constraint(bits, pltpu.HBM), groups)
     dither, rotated, peaks = lax.optimization_barrier((dither, rotated, peaks))
     peaks = lax.all_to_all(peaks, axes, 0, 0, tiled=True)
-    symbols, scales = encode(rotated, dither[0, 0], peaks, layout.reshape(1, blocks), levels)
-    received = lax.all_to_all(symbols.reshape(groups, owned, block), axes, 0, 0, tiled=True)
+    mine, others, scales = encode(core, rotated, dither[0, 0], peaks, layout.reshape(1, blocks), levels)
+    merged = merge(levels, mine, lax.ppermute(others, core, OTHER_CORE))
+    pairs = merged.astype(jnp.float16).reshape(groups // 2, owned, block)
+    pairs = lax.all_to_all(pairs, chips, 0, 0, tiled=True)
+    total = jnp.sum(pairs.astype(jnp.float32), axis=0)
     place = lax.axis_index(axes).reshape(1)
     new_master, new_moment, new_second, copies = owner(
-        place, levels, received, scales, bits, master[0], first_moment[0], second_moment[0], groups // 2
+        place, total, scales, bits, master[0], first_moment[0], second_moment[0], groups // 2
     )
     mine = lax.all_to_all(copies, chips, 0, 0, tiled=True)
     others = lax.ppermute(mine, core, OTHER_CORE)

time: 96.2 us -> 89.4 us (0.929)
  waiting for transfers between devices: 30.3 us -> 20.8 us
  starting transfers between devices: 6.13 us -> 7.61 us
  other arithmetic: 0 us -> 1.24 us
    all_to_all x1, waiting for transfers between devices: 28.4 us -> 16.5 us  [local(): pairs = lax.all_to_all(pairs, chips, 0, 0, tiled=True)]
    pallas_call x1 -> x2, Pallas kernels: 8.94 us -> 14.7 us  [the longest x1 7.87 us: encode(): pl.pallas_call(functools.partial(encode_kernel, core), grid=(block // col...]
    pallas_call x1, Pallas kernels: 6.89 us -> 1.32 us  [owner(): pl.pallas_call(owner_kernel, grid_spec=pltpu.PrefetchScalarGridSpec(num_s...]
    ppermute x0 -> x1, waiting for transfers between devices: none -> 2.29 us  [local(): merged = merge(levels, mine, lax.ppermute(others, core, OTHER_CORE))]
    ppermute x1, starting transfers between devices: 1.92 us -> 3.34 us  [local(): others = lax.ppermute(mine, core, OTHER_CORE)]
    reshape x0 -> x1, other arithmetic: none -> 1.09 us  [local(): pairs = merged.astype(jnp.float16).reshape(groups // 2, owned, block)]
  transfers between devices with their start and end apart: 2 -> 3, of which waited for: 2 -> 3; matrix products, arithmetic and copies ran while one was open for 0% -> 0% of each run, Pallas kernels for 0% -> 0%
where the time goes in v4:
time: 89.4 us; the launch traced here: 89.1 us
  blocking collectives  34.6 us (39%)
  Pallas kernels  23.8 us (27%)
  waiting for transfers between devices  20.8 us (23%)
  starting transfers between devices  7.61 us (9%)
  other arithmetic  1.24 us (1%)
    all_to_all x1, blocking collectives, local(): mine = lax.all_to_all(copies, chips, 0, 0, tiled=True)  18.5 us
    all_to_all x1, waiting for transfers between devices, local(): pairs = lax.all_to_all(pairs, chips, 0, 0, tiled=True)  16.5 us
    all_to_all x1, blocking collectives, local(): peaks = lax.all_to_all(peaks, axes, 0, 0, tiled=True)  16.1 us
    pallas_call x1, Pallas kernels, encode(): pl.pallas_call(functools.partial(encode_kernel, core), grid=(block // col...  7.87 us
    pallas_call x1, Pallas kernels, merge(): pl.pallas_call(merge_kernel, in_specs=[pl.BlockSpec(memory_space=pltpu.SM...  6.8 us
    pallas_call x1, Pallas kernels, rotate(): pl.pallas_call(rotate_kernel, grid=(blocks // rows,), in_specs=[pl.BlockS...  5.32 us
    all_to_all x1, starting transfers between devices, local(): pairs = lax.all_to_all(pairs, chips, 0, 0, tiled=True)  3.8 us
    ppermute x1, starting transfers between devices, local(): others = lax.ppermute(mine, core, OTHER_CORE)  3.34 us
  transfers between devices with their start and end apart: 3, of which 3 were waited for; matrix products, arithmetic and copies ran while one was open for 0% of the time, Pallas kernels for 0%

profile of v4, /device:TPU:1, one launch (start us, length us, event | category | flops | bytes accessed | tf_op | source)
XLA Modules:
  0.0 89.1 jit_solution(12573062924820289319)
XLA Ops:
  0.6 0.0 copy-start
  0.6 0.0 copy-start.5
  0.7 0.0 copy-start.6
  0.7 5.3 %rotate.1 = (f32[256,4096]{1,0:T(8,128)S(1)}, f32[32,8,128]{2,1,0:T(8,128)S(1)}) custom-call(f32[256,4096]{1,0:T(8,128)} %bitcast.25, s32[1,4096]{1,0:T(1,128)} %bitcast.22), custom_call_target="tpu_custom_call" | custom-call | tf_op jit(solution)/shard_map/rotate/pallas_call | solution.py:105
  6.0 16.1 %all_to_all.15.peaks_ref = f32[32,8,128]{2,1,0:T(8,128)S(1)} all-to-all(f32[32,8,128]{2,1,0:T(8,128)S(1)} %get-tuple-element.20), channel_id=1, replica_groups=mesh['section'=4,'dp_chip'=16,'dp_core'=2] {'dp_chip','dp_core'}, dimensions={0} | all-to-all | bytes 262144 | tf_op jit(solution)/shard_map/all_to_all | solution.py:400
  22.1 0.0 copy-done
  22.1 0.0 copy-done.5
  22.1 0.0 copy-done.6
  22.1 7.9 %encode.1 = (bf16[128,4096]{1,0:T(8,128)(2,1)S(1)}, bf16[128,4096]{1,0:T(8,128)(2,1)S(1)}, f32[256,128]{1,0:T(8,128)S(1)}) custom-call(f32[16]{0:T(128)S(1)} %copy-done.6, f32[256,4096]{1,0:T(8,128)S(1)} %get-tuple-element.18.rotated_ref, s32[256,4096]{1,0:T(8,128)S(1)} %bitcast.17, f32[32,8,128]{2,1,0:T(8,128)S(1)} %all_to_all.15.peaks_ref, ...), custom_call_target="tpu_custom_call" | custom-call | tf_op jit(solution)/shard_map/encode/pallas_call | solution.py:242
  30.0 0.5 collective-permute-start
  30.4 2.3 %collective-permute-done.theirs_ref = bf16[128,4096]{1,0:T(8,128)(2,1)S(1)} collective-permute-done((bf16[128,4096]{1,0:T(8,128)(2,1)S(1)}, bf16[128,4096]{1,0:T(8,128)(2,1)S(1)}, u32[]{:S(2)}, u32[]{:S(2)}) %collective-permute-start) | collective-permute-done | bytes 1048608 | tf_op jit(solution)/shard_map/ppermute | solution.py:402
  32.7 6.8 %merge.1 = f32[128,4096]{1,0:T(8,128)S(1)} custom-call(f32[16]{0:T(128)S(1)} %copy-done.6, bf16[128,4096]{1,0:T(8,128)(2,1)S(1)} %get-tuple-element.21.mine_ref, bf16[128,4096]{1,0:T(8,128)(2,1)S(1)} %collective-permute-done.theirs_ref), custom_call_target="tpu_custom_call" | custom-call | tf_op jit(solution)/shard_map/merge/pallas_call | solution.py:298
  39.5 1.1 %convert_bitcast_fusion = f16[16,8,4096]{2,1,0:T(8,128)(2,1)} fusion(f32[128,4096]{1,0:T(8,128)S(1)} %merge.1), kind=kLoop, calls=%fused_computation.1 | loop fusion | flops 524288 | bytes 3145728 | tf_op jit(solution)/shard_map/reshape | solution.py:403
  40.6 0.0 copy-start.1
  40.6 0.0 copy-start.2
  40.6 0.0 copy-start.3
  40.6 0.0 copy-start.4
  40.6 3.8 %all-to-all-start.1 = ((f16[16,8,4096]{2,1,0:T(8,128)(2,1)}), f16[16,8,4096]{2,1,0:T(8,128)(2,1)S(1)}, u32[]{:S(2)}, u32[]{:S(2)}) async-start(f16[16,8,4096]{2,1,0:T(8,128)(2,1)} %convert_bitcast_fusion), calls=%async_computation.1 | async-start | bytes 2097152 | tf_op jit(solution)/shard_map/all_to_all | solution.py:404
  44.5 16.5 %all-to-all-done.1 = f16[16,8,4096]{2,1,0:T(8,128)(2,1)S(1)} async-done(((f16[16,8,4096]{2,1,0:T(8,128)(2,1)}), f16[16,8,4096]{2,1,0:T(8,128)(2,1)S(1)}, u32[]{:S(2)}, u32[]{:S(2)}) %all-to-all-start.1) | async-done | bytes 1048608 | tf_op jit(solution)/shard_map/all_to_all | solution.py:404
  61.0 0.1 convert_reduce_fusion.total_ref
  61.1 0.0 copy-done.1
  61.1 0.0 copy-done.2
  61.2 0.0 copy-done.3
  61.2 0.0 copy-done.4
  61.2 1.3 %owner.1 = (f32[8,4096]{1,0:T(8,128)}, f32[8,4096]{1,0:T(8,128)}, f32[8,4096]{1,0:T(8,128)}, bf16[16,8,4096]{2,1,0:T(8,128)(2,1)S(1)}) custom-call(s32[1]{0:T(128)} %bitcast.place_ref, f32[8,4096]{1,0:T(8,128)S(1)} %convert_reduce_fusion.total_ref, f32[256,128]{1,0:T(8,128)S(1)} %get-tuple-element.23.scales_ref, s32[1,4096]{1,0:T(1,128)S(1)} %bitcast.23, ...), custom_call_target="tpu_custom_call" | custom-call | tf_op jit(solution)/shard_map/owner/pallas_call | solution.py:338
  62.5 18.5 %all_to_all.16 = bf16[16,8,4096]{2,1,0:T(8,128)(2,1)S(1)} all-to-all(bf16[16,8,4096]{2,1,0:T(8,128)(2,1)S(1)} %get-tuple-element.27), channel_id=1, replica_groups=mesh['section'=4,'dp_chip'=16,'dp_core'=2] {'dp_chip'}, dimensions={0} | all-to-all | bytes 2097152 | tf_op jit(solution)/shard_map/all_to_all | solution.py:410
  81.0 3.3 %collective-permute-start.1 = (bf16[16,8,4096]{2,1,0:T(8,128)(2,1)S(1)}, bf16[16,8,4096]{2,1,0:T(8,128)(2,1)S(1)}, u32[]{:S(2)}, u32[]{:S(2)}) collective-permute-start(bf16[16,8,4096]{2,1,0:T(8,128)(2,1)S(1)} %all_to_all.16), channel_id=1, source_target_pairs={{0,1},{1,0},{2,3},{3,2},{4,5},{5,4},{6,7},{7,6},{8,9},{9,8},{10,11... | collective-permute-start | bytes 3145736 | tf_op jit(solution)/shard_map/ppermute | solution.py:411
  84.3 0.1 reshape.43
  84.4 0.1 dynamic-slice_reduce_fusion
  84.5 0.1 reshape.44.my_slots_ref
  84.6 0.1 reshape.45.other_slots_ref
  84.7 1.9 %collective-permute-done.1 = bf16[16,8,4096]{2,1,0:T(8,128)(2,1)S(1)} collective-permute-done((bf16[16,8,4096]{2,1,0:T(8,128)(2,1)S(1)}, bf16[16,8,4096]{2,1,0:T(8,128)(2,1)S(1)}, u32[]{:S(2)}, u32[]{:S(2)}) %collective-permute-start.1) | collective-permute-done | bytes 1048608 | tf_op jit(solution)/shard_map/ppermute | solution.py:411
  86.6 2.5 %reorder.1 = bf16[256,4096]{1,0:T(8,128)(2,1)} custom-call(bf16[128,4096]{1,0:T(8,128)(2,1)S(1)} %bitcast.16, bf16[128,4096]{1,0:T(8,128)(2,1)S(1)} %bitcast.18, s32[1,128]{1,0:T(1,128)S(1)} %reshape.44.my_slots_ref, s32[1,128]{1,0:T(1,128)S(1)} %reshape.45.other_slots_ref), custom_call_target="tpu_custom_call" | custom-call | tf_op jit(solution)/shard_map/reorder/pallas_call | solution.py:376
Async XLA Ops:
  0.6 21.5 %copy-start = (s32[1,1,256,4096]{3,2,1,0:T(8,128)S(1)}, s32[1,1,256,4096]{3,2,1,0:T(8,128)}, u32[]{:S(2)}) copy-start(s32[1,1,256,4096]{3,2,1,0:T(8,128)} %param.9) | copy-start | bytes 12582916
  0.6 21.4 %copy-start.5 = (s32[256]{0:T(256)S(1)}, s32[256]{0:T(256)}, u32[]{:S(2)}) copy-start(s32[256]{0:T(256)} %param.12) | copy-start | bytes 3076
  0.7 21.4 %copy-start.6 = (f32[16]{0:T(128)S(1)}, f32[16]{0:T(128)}, u32[]{:S(2)}) copy-start(f32[16]{0:T(128)} %levels_ref.3) | copy-start | bytes 196
  30.0 2.8 %collective-permute-start = (bf16[128,4096]{1,0:T(8,128)(2,1)S(1)}, bf16[128,4096]{1,0:T(8,128)(2,1)S(1)}, u32[]{:S(2)}, u32[]{:S(2)}) collective-permute-start(bf16[128,4096]{1,0:T(8,128)(2,1)S(1)} %get-tuple-element.22), channel_id=1, source_target_pairs={{0,1},{1,0},{2,3},{3,2},{4,5},{5,4},{6,7},{7,6},{8,9},{9,8},{10,11... | collective-permute-start | bytes 3145736 | tf_op jit(solution)/shard_map/ppermute | solution.py:402
  40.6 20.5 %copy-start.1 = (f32[1,8,4096]{2,1,0:T(8,128)S(1)}, f32[1,8,4096]{2,1,0:T(8,128)}, u32[]{:S(2)}) copy-start(f32[1,8,4096]{2,1,0:T(8,128)} %param.13) | copy-start | bytes 393220
  40.6 20.5 %copy-start.2 = (f32[1,8,4096]{2,1,0:T(8,128)S(1)}, f32[1,8,4096]{2,1,0:T(8,128)}, u32[]{:S(2)}) copy-start(f32[1,8,4096]{2,1,0:T(8,128)} %param.14) | copy-start | bytes 393220
  40.6 20.5 %copy-start.3 = (f32[1,8,4096]{2,1,0:T(8,128)S(1)}, f32[1,8,4096]{2,1,0:T(8,128)}, u32[]{:S(2)}) copy-start(f32[1,8,4096]{2,1,0:T(8,128)} %param.15) | copy-start | bytes 393220
  40.6 20.5 %copy-start.4 = (s32[4096]{0:T(1024)S(1)}, s32[4096]{0:T(1024)}, u32[]{:S(2)}) copy-start(s32[4096]{0:T(1024)} %param.10) | copy-start | bytes 49156
  40.6 20.3 %all-to-all-start.1 = ((f16[16,8,4096]{2,1,0:T(8,128)(2,1)}), f16[16,8,4096]{2,1,0:T(8,128)(2,1)S(1)}, u32[]{:S(2)}, u32[]{:S(2)}) async-start(f16[16,8,4096]{2,1,0:T(8,128)(2,1)} %convert_bitcast_fusion), calls=%async_computation.1 | async-start | bytes 2097152 | tf_op jit(solution)/shard_map/all_to_all | solution.py:404
  81.0 5.6 %collective-permute-start.1 = (bf16[16,8,4096]{2,1,0:T(8,128)(2,1)S(1)}, bf16[16,8,4096]{2,1,0:T(8,128)(2,1)S(1)}, u32[]{:S(2)}, u32[]{:S(2)}) collective-permute-start(bf16[16,8,4096]{2,1,0:T(8,128)(2,1)S(1)} %all_to_all.16), channel_id=1, source_target_pairs={{0,1},{1,0},{2,3},{3,2},{4,5},{5,4},{6,7},{7,6},{8,9},{9,8},{10,11... | collective-permute-start | bytes 3145736 | tf_op jit(solution)/shard_map/ppermute | solution.py:411

commit v5 on v4

--- a/solution.py
+++ b/solution.py
@@ -19,6 +19,7 @@
 CELLS = 64
 CELL_RATE = 31.95
 MIB = 1024 * 1024
+TABLE_EVERY = 2
 VMEM_BYTES = 16 * MIB
 OTHER_CORE = ((0, 1), (1, 0))
 
@@ -271,38 +272,77 @@
     )(levels, rotated, dither, peaks, layout)
 
 
-def merge_kernel(levels_ref, mine_ref, theirs_ref, out_ref):
+def decode_tables(levels_ref):
+    count = levels_ref.shape[0]
+    lane = lax.broadcasted_iota(jnp.int32, (8, LANES), 1)
+    slope = jnp.zeros((8, LANES), jnp.float32)
+    intercept = jnp.full((8, LANES), levels_ref[count - 1], jnp.float32)
+    for number in range(count - 1):
+        low = jnp.full((8, LANES), levels_ref[number], jnp.float32)
+        spacing = jnp.full((8, LANES), levels_ref[number + 1], jnp.float32) - low
+        slope = jnp.where(lane == number, spacing, slope)
+        intercept = jnp.where(lane == number, low - number * spacing, intercept)
+    return slope, intercept
+
+
+def decode_kernel(levels_ref, symbols_ref, *refs):
+    out_ref = refs[-1]
     count = levels_ref.shape[0]
     rows, block = out_ref.shape
-    wide = 1024
+    wide, deep = 1024, 64
+    slope, intercept = decode_tables(levels_ref)
     spacings = [levels_ref[level + 1] - levels_ref[level] for level in range(count - 1)]
     weights = [spacings[0]] + [spacings[level] - spacings[level - 1] for level in range(1, count - 1)] + [-spacings[-1]]
 
     def some(number, carry):
-        here = pl.ds(pl.multiple_of(number // (block // wide) * 16, 16), 16)
+        down = pl.multiple_of(number // (block // wide) * deep, deep)
         start = number % (block // wide) * wide
+        places, tiles = [], []
         for part in range(wide // LANES):
-            there = pl.ds(pl.multiple_of(start + part * LANES, LANES), LANES)
-            one, two = mine_ref[here, there].astype(jnp.float32), theirs_ref[here, there].astype(jnp.float32)
-            total = jnp.full((16, LANES), 2.0 * levels_ref[count - 1], jnp.float32)
-            for level in range(count):
-                total = total + weights[level] * (jnp.maximum(one, float(level)) + jnp.maximum(two, float(level)))
-            out_ref[here, there] = total
+            for row in range(0, deep, 16):
+                place = (
+                    pl.ds(pl.multiple_of(down + row, 16), 16),
+                    pl.ds(pl.multiple_of(start + part * LANES, LANES), LANES),
+                )
+                symbols = symbols_ref[place].astype(jnp.float32)
+                places.append(place)
+                tiles += [symbols[:8], symbols[8:]]
+        by_table = [at % TABLE_EVERY == 1 for at in range(len(tiles))]
+        bounded = {
+            at: jnp.minimum(jnp.maximum(tile, 0.0), count - 1.0) for at, tile in enumerate(tiles) if by_table[at]
+        }
+        index = {at: tile.astype(jnp.int32) for at, tile in bounded.items()}
+        lines = {at: (looked_up(slope, which), looked_up(intercept, which)) for at, which in index.items()}
+        values = []
+        for at, tile in enumerate(tiles):
+            if by_table[at]:
+                value = bounded[at] * lines[at][0] + lines[at][1]
+            else:
+                value = jnp.full((8, LANES), levels_ref[count - 1], jnp.float32)
+                for level in range(count):
+                    value = value + weights[level] * jnp.maximum(tile, float(level))
+            values.append(value)
+        for at, place in enumerate(places):
+            value = jnp.concatenate(values[2 * at : 2 * at + 2], axis=0)
+            for ref in refs[:-1]:
+                value = value + ref[place]
+            out_ref[place] = value
         return carry
 
-    lax.fori_loop(0, rows // 16 * (block // wide), some, 0)
-
-
-def merge(levels, mine, theirs):
+    lax.fori_loop(0, rows // deep * (block // wide), some, 0)
+
+
+def decode(levels, symbols, *others):
     here = pl.BlockSpec(memory_space=pltpu.VMEM)
     return pl.pallas_call(
-        merge_kernel,
-        in_specs=[pl.BlockSpec(memory_space=pltpu.SMEM), here, here],
+        decode_kernel,
+        in_specs=[pl.BlockSpec(memory_space=pltpu.SMEM), here] + [here] * len(others),
         out_specs=here,
-        out_shape=pltpu.VMEM(mine.shape, jnp.float32),
+        out_shape=pltpu.VMEM(symbols.shape, jnp.float32),
         compiler_params=pltpu.CompilerParams(vmem_limit_bytes=VMEM_BYTES),
-        name="merge",
-    )(levels, mine, theirs)
+        cost_estimate=pl.CostEstimate(flops=48 * symbols.size, bytes_accessed=6 * symbols.size, transcendentals=0),
+        name="decode",
+    )(levels, symbols, *others)
 
 
 def owner_kernel(
@@ -399,7 +439,8 @@
     dither, rotated, peaks = lax.optimization_barrier((dither, rotated, peaks))
     peaks = lax.all_to_all(peaks, axes, 0, 0, tiled=True)
     mine, others, scales = encode(core, rotated, dither[0, 0], peaks, layout.reshape(1, blocks), levels)
-    merged = merge(levels, mine, lax.ppermute(others, core, OTHER_CORE))
+    theirs = lax.ppermute(others, core, OTHER_CORE)
+    merged = decode(levels, theirs, decode(levels, mine))
     pairs = merged.astype(jnp.float16).reshape(groups // 2, owned, block)
     pairs = lax.all_to_all(pairs, chips, 0, 0, tiled=True)
     total = jnp.sum(pairs.astype(jnp.float32), axis=0)

time: 89.4 us -> 86.2 us (0.964)
  Pallas kernels: 23.8 us -> 22.5 us
  waiting for transfers between devices: 20.8 us -> 19.7 us
  blocking collectives: 34.6 us -> 33.6 us
    ppermute x1, waiting for transfers between devices: 2.29 us -> 0.01 us  [local(): theirs = lax.ppermute(others, core, OTHER_CORE)]
    pallas_call x1 -> x2, Pallas kernels: 6.8 us -> 5.53 us  [decode(): pl.pallas_call(decode_kernel, in_specs=[pl.BlockSpec(memory_space=pltpu.S...]
    all_to_all x1, waiting for transfers between devices: 16.5 us -> 17.7 us  [local(): pairs = lax.all_to_all(pairs, chips, 0, 0, tiled=True)]
    all_to_all x1, blocking collectives: 18.5 us -> 17.5 us  [local(): mine = lax.all_to_all(copies, chips, 0, 0, tiled=True)]
  transfers between devices with their start and end apart: 3 -> 3, of which waited for: 3 -> 2; matrix products, arithmetic and copies ran while one was open for 0% -> 0% of each run, Pallas kernels for 0% -> 3%
where the time goes in v5:
time: 86.2 us; the launch traced here: 85.9 us
  blocking collectives  33.6 us (39%)
  Pallas kernels  22.5 us (26%)
  waiting for transfers between devices  19.7 us (23%)
  starting transfers between devices  7.73 us (9%)
  other arithmetic  1.24 us (1%)
    all_to_all x1, waiting for transfers between devices, local(): pairs = lax.all_to_all(pairs, chips, 0, 0, tiled=True)  17.7 us
    all_to_all x1, blocking collectives, local(): mine = lax.all_to_all(copies, chips, 0, 0, tiled=True)  17.5 us
    all_to_all x1, blocking collectives, local(): peaks = lax.all_to_all(peaks, axes, 0, 0, tiled=True)  16.1 us
    pallas_call x1, Pallas kernels, encode(): pl.pallas_call(functools.partial(encode_kernel, core), grid=(block // col...  7.87 us
    pallas_call x2, Pallas kernels, decode(): pl.pallas_call(decode_kernel, in_specs=[pl.BlockSpec(memory_space=pltpu.S...  5.53 us
    pallas_call x1, Pallas kernels, rotate(): pl.pallas_call(rotate_kernel, grid=(blocks // rows,), in_specs=[pl.BlockS...  5.32 us
    all_to_all x1, starting transfers between devices, local(): pairs = lax.all_to_all(pairs, chips, 0, 0, tiled=True)  3.8 us
    ppermute x1, starting transfers between devices, local(): others = lax.ppermute(mine, core, OTHER_CORE)  3.46 us
  transfers between devices with their start and end apart: 3, of which 2 were waited for; matrix products, arithmetic and copies ran while one was open for 0% of the time, Pallas kernels for 3%

profile of v5, /device:TPU:1, one launch (start us, length us, event | category | flops | bytes accessed | tf_op | source)
XLA Modules:
  0.0 85.9 jit_solution(8233653583095931958)
XLA Ops:
  0.6 0.0 copy-start
  0.6 0.0 copy-start.5
  0.7 0.0 copy-start.6
  0.7 5.3 %rotate.1 = (f32[256,4096]{1,0:T(8,128)S(1)}, f32[32,8,128]{2,1,0:T(8,128)S(1)}) custom-call(f32[256,4096]{1,0:T(8,128)} %bitcast.25, s32[1,4096]{1,0:T(1,128)} %bitcast.22), custom_call_target="tpu_custom_call" | custom-call | tf_op jit(solution)/shard_map/rotate/pallas_call | solution.py:106
  6.0 16.1 %all_to_all.15.peaks_ref = f32[32,8,128]{2,1,0:T(8,128)S(1)} all-to-all(f32[32,8,128]{2,1,0:T(8,128)S(1)} %get-tuple-element.20), channel_id=1, replica_groups=mesh['section'=4,'dp_chip'=16,'dp_core'=2] {'dp_chip','dp_core'}, dimensions={0} | all-to-all | bytes 262144 | tf_op jit(solution)/shard_map/all_to_all | solution.py:440
  22.1 0.0 copy-done
  22.1 0.0 copy-done.5
  22.1 0.0 copy-done.6
  22.1 7.9 %encode.1 = (bf16[128,4096]{1,0:T(8,128)(2,1)S(1)}, bf16[128,4096]{1,0:T(8,128)(2,1)S(1)}, f32[256,128]{1,0:T(8,128)S(1)}) custom-call(f32[16]{0:T(128)S(1)} %copy-done.5, f32[256,4096]{1,0:T(8,128)S(1)} %get-tuple-element.18.rotated_ref, s32[256,4096]{1,0:T(8,128)S(1)} %bitcast.17, f32[32,8,128]{2,1,0:T(8,128)S(1)} %all_to_all.15.peaks_ref, ...), custom_call_target="tpu_custom_call" | custom-call | tf_op jit(solution)/shard_map/encode/pallas_call | solution.py:243
  30.0 0.5 collective-permute-start
  30.4 2.8 %decode.2.refs_0_ = f32[128,4096]{1,0:T(8,128)S(1)} custom-call(f32[16]{0:T(128)S(1)} %copy-done.5, bf16[128,4096]{1,0:T(8,128)(2,1)S(1)} %get-tuple-element.22.symbols_ref), custom_call_target="tpu_custom_call" | custom-call | flops 25165824 | bytes 3145728 | tf_op jit(solution)/shard_map/decode/pallas_call | solution.py:337
  33.3 0.0 collective-permute-done.symbols_ref
  33.3 2.7 %decode.3 = f32[128,4096]{1,0:T(8,128)S(1)} custom-call(f32[16]{0:T(128)S(1)} %copy-done.5, bf16[128,4096]{1,0:T(8,128)(2,1)S(1)} %collective-permute-done.symbols_ref, f32[128,4096]{1,0:T(8,128)S(1)} %decode.2.refs_0_), custom_call_target="tpu_custom_call" | custom-call | flops 25165824 | bytes 3145728 | tf_op jit(solution)/shard_map/decode/pallas_call | solution.py:337
  36.0 1.1 %convert_bitcast_fusion = f16[16,8,4096]{2,1,0:T(8,128)(2,1)} fusion(f32[128,4096]{1,0:T(8,128)S(1)} %decode.3), kind=kLoop, calls=%fused_computation.1 | loop fusion | flops 524288 | bytes 3145728 | tf_op jit(solution)/shard_map/reshape | solution.py:444
  37.1 0.0 copy-start.1
  37.1 0.0 copy-start.2
  37.1 0.0 copy-start.3
  37.1 0.0 copy-start.4
  37.1 3.8 %all-to-all-start.1 = ((f16[16,8,4096]{2,1,0:T(8,128)(2,1)}), f16[16,8,4096]{2,1,0:T(8,128)(2,1)S(1)}, u32[]{:S(2)}, u32[]{:S(2)}) async-start(f16[16,8,4096]{2,1,0:T(8,128)(2,1)} %convert_bitcast_fusion), calls=%async_computation.1 | async-start | bytes 2097152 | tf_op jit(solution)/shard_map/all_to_all | solution.py:445
  40.9 17.7 %all-to-all-done.1 = f16[16,8,4096]{2,1,0:T(8,128)(2,1)S(1)} async-done(((f16[16,8,4096]{2,1,0:T(8,128)(2,1)}), f16[16,8,4096]{2,1,0:T(8,128)(2,1)S(1)}, u32[]{:S(2)}, u32[]{:S(2)}) %all-to-all-start.1) | async-done | bytes 1048608 | tf_op jit(solution)/shard_map/all_to_all | solution.py:445
  58.6 0.1 convert_reduce_fusion.total_ref
  58.8 0.0 copy-done.1
  58.8 0.0 copy-done.2
  58.8 0.0 copy-done.3
  58.8 0.0 copy-done.4
  58.8 1.3 %owner.1 = (f32[8,4096]{1,0:T(8,128)}, f32[8,4096]{1,0:T(8,128)}, f32[8,4096]{1,0:T(8,128)}, bf16[16,8,4096]{2,1,0:T(8,128)(2,1)S(1)}) custom-call(s32[1]{0:T(128)} %bitcast.place_ref, f32[8,4096]{1,0:T(8,128)S(1)} %convert_reduce_fusion.total_ref, f32[256,128]{1,0:T(8,128)S(1)} %get-tuple-element.23.scales_ref, s32[1,4096]{1,0:T(1,128)S(1)} %bitcast.23, ...), custom_call_target="tpu_custom_call" | custom-call | tf_op jit(solution)/shard_map/owner/pallas_call | solution.py:378
  60.1 17.5 %all_to_all.16 = bf16[16,8,4096]{2,1,0:T(8,128)(2,1)S(1)} all-to-all(bf16[16,8,4096]{2,1,0:T(8,128)(2,1)S(1)} %get-tuple-element.27), channel_id=1, replica_groups=mesh['section'=4,'dp_chip'=16,'dp_core'=2] {'dp_chip'}, dimensions={0} | all-to-all | bytes 2097152 | tf_op jit(solution)/shard_map/all_to_all | solution.py:451
  77.6 3.5 %collective-permute-start.1 = (bf16[16,8,4096]{2,1,0:T(8,128)(2,1)S(1)}, bf16[16,8,4096]{2,1,0:T(8,128)(2,1)S(1)}, u32[]{:S(2)}, u32[]{:S(2)}) collective-permute-start(bf16[16,8,4096]{2,1,0:T(8,128)(2,1)S(1)} %all_to_all.16), channel_id=1, source_target_pairs={{0,1},{1,0},{2,3},{3,2},{4,5},{5,4},{6,7},{7,6},{8,9},{9,8},{10,11... | collective-permute-start | bytes 3145736 | tf_op jit(solution)/shard_map/ppermute | solution.py:452
  81.1 0.1 reshape.43
  81.2 0.1 dynamic-slice_reduce_fusion
  81.2 0.1 reshape.44.my_slots_ref
  81.3 0.1 reshape.45.other_slots_ref
  81.4 1.9 %collective-permute-done.1 = bf16[16,8,4096]{2,1,0:T(8,128)(2,1)S(1)} collective-permute-done((bf16[16,8,4096]{2,1,0:T(8,128)(2,1)S(1)}, bf16[16,8,4096]{2,1,0:T(8,128)(2,1)S(1)}, u32[]{:S(2)}, u32[]{:S(2)}) %collective-permute-start.1) | collective-permute-done | bytes 1048608 | tf_op jit(solution)/shard_map/ppermute | solution.py:452
  83.3 2.5 %reorder.1 = bf16[256,4096]{1,0:T(8,128)(2,1)} custom-call(bf16[128,4096]{1,0:T(8,128)(2,1)S(1)} %bitcast.16, bf16[128,4096]{1,0:T(8,128)(2,1)S(1)} %bitcast.18, s32[1,128]{1,0:T(1,128)S(1)} %reshape.44.my_slots_ref, s32[1,128]{1,0:T(1,128)S(1)} %reshape.45.other_slots_ref), custom_call_target="tpu_custom_call" | custom-call | tf_op jit(solution)/shard_map/reorder/pallas_call | solution.py:416
Async XLA Ops:
  0.6 21.5 %copy-start = (s32[1,1,256,4096]{3,2,1,0:T(8,128)S(1)}, s32[1,1,256,4096]{3,2,1,0:T(8,128)}, u32[]{:S(2)}) copy-start(s32[1,1,256,4096]{3,2,1,0:T(8,128)} %param.9) | copy-start | bytes 12582916
  0.6 21.4 %copy-start.5 = (f32[16]{0:T(128)S(1)}, f32[16]{0:T(128)}, u32[]{:S(2)}) copy-start(f32[16]{0:T(128)} %levels_ref.5) | copy-start | bytes 196
  0.7 21.4 %copy-start.6 = (s32[256]{0:T(256)S(1)}, s32[256]{0:T(256)}, u32[]{:S(2)}) copy-start(s32[256]{0:T(256)} %param.12) | copy-start | bytes 3076
  30.0 3.3 %collective-permute-start = (bf16[128,4096]{1,0:T(8,128)(2,1)S(1)}, bf16[128,4096]{1,0:T(8,128)(2,1)S(1)}, u32[]{:S(2)}, u32[]{:S(2)}) collective-permute-start(bf16[128,4096]{1,0:T(8,128)(2,1)S(1)} %get-tuple-element.21), channel_id=1, source_target_pairs={{0,1},{1,0},{2,3},{3,2},{4,5},{5,4},{6,7},{7,6},{8,9},{9,8},{10,11... | collective-permute-start | bytes 3145736 | tf_op jit(solution)/shard_map/ppermute | solution.py:442
  37.1 21.7 %copy-start.1 = (f32[1,8,4096]{2,1,0:T(8,128)S(1)}, f32[1,8,4096]{2,1,0:T(8,128)}, u32[]{:S(2)}) copy-start(f32[1,8,4096]{2,1,0:T(8,128)} %param.13) | copy-start | bytes 393220
  37.1 21.7 %copy-start.2 = (f32[1,8,4096]{2,1,0:T(8,128)S(1)}, f32[1,8,4096]{2,1,0:T(8,128)}, u32[]{:S(2)}) copy-start(f32[1,8,4096]{2,1,0:T(8,128)} %param.14) | copy-start | bytes 393220
  37.1 21.7 %copy-start.3 = (f32[1,8,4096]{2,1,0:T(8,128)S(1)}, f32[1,8,4096]{2,1,0:T(8,128)}, u32[]{:S(2)}) copy-start(f32[1,8,4096]{2,1,0:T(8,128)} %param.15) | copy-start | bytes 393220
  37.1 21.7 %copy-start.4 = (s32[4096]{0:T(1024)S(1)}, s32[4096]{0:T(1024)}, u32[]{:S(2)}) copy-start(s32[4096]{0:T(1024)} %param.10) | copy-start | bytes 49156
  37.1 21.5 %all-to-all-start.1 = ((f16[16,8,4096]{2,1,0:T(8,128)(2,1)}), f16[16,8,4096]{2,1,0:T(8,128)(2,1)S(1)}, u32[]{:S(2)}, u32[]{:S(2)}) async-start(f16[16,8,4096]{2,1,0:T(8,128)(2,1)} %convert_bitcast_fusion), calls=%async_computation.1 | async-start | bytes 2097152 | tf_op jit(solution)/shard_map/all_to_all | solution.py:445
  77.6 5.7 %collective-permute-start.1 = (bf16[16,8,4096]{2,1,0:T(8,128)(2,1)S(1)}, bf16[16,8,4096]{2,1,0:T(8,128)(2,1)S(1)}, u32[]{:S(2)}, u32[]{:S(2)}) collective-permute-start(bf16[16,8,4096]{2,1,0:T(8,128)(2,1)S(1)} %all_to_all.16), channel_id=1, source_target_pairs={{0,1},{1,0},{2,3},{3,2},{4,5},{5,4},{6,7},{7,6},{8,9},{9,8},{10,11... | collective-permute-start | bytes 3145736 | tf_op jit(solution)/shard_map/ppermute | solution.py:452

commit v6 on v5

--- a/solution.py
+++ b/solution.py
@@ -96,13 +96,13 @@
         lines = [
             jnp.max(jnp.transpose(rows_ref[at : at + LANES, :]), axis=0, keepdims=True) for at in range(0, blocks, LANES)
         ]
-        lines = jnp.concatenate(lines * (8 // len(lines)), axis=0)
+        lines = jnp.concatenate(lines, axis=0)
         peaks_ref[...] = jnp.broadcast_to(lines[None], peaks_ref.shape)
 
 
 def rotate(gradient, bits, groups):
     blocks, block = gradient.shape
-    rows = 64
+    rows = 128
     return pl.pallas_call(
         rotate_kernel,
         grid=(blocks // rows,),
@@ -112,11 +112,11 @@
         ],
         out_specs=[
             pl.BlockSpec((rows, block), lambda i: (i, 0)),
-            pl.BlockSpec((groups, 8, LANES), lambda i: (0, 0, 0)),
+            pl.BlockSpec((groups, blocks // LANES, LANES), lambda i: (0, 0, 0)),
         ],
         out_shape=[
             jax.ShapeDtypeStruct((blocks, block), jnp.float32),
-            jax.ShapeDtypeStruct((groups, 8, LANES), jnp.float32),
+            jax.ShapeDtypeStruct((groups, blocks // LANES, LANES), jnp.float32),
         ],
         scratch_shapes=[pltpu.VMEM((3 * WIDE, WIDE), jnp.bfloat16), pltpu.VMEM((blocks, LANES), jnp.float32)],
         compiler_params=pltpu.CompilerParams(vmem_limit_bytes=49 * MIB),
@@ -189,7 +189,7 @@
             lines_ref[2 * number + 1] = intercept
 
     threshold, slope, intercept = tables_ref[0], tables_ref[1], tables_ref[2]
-    deep = 128
+    deep = 64
 
     def some_rows(number, carry):
         start = pl.multiple_of(number * deep, deep)
@@ -239,7 +239,7 @@
 
 def encode(core, rotated, dither, peaks, layout, levels):
     blocks, block = rotated.shape
-    columns = 1024
+    columns = 2048
     return pl.pallas_call(
         functools.partial(encode_kernel, core),
         grid=(block // columns,),
@@ -398,21 +398,25 @@
     )(place, total, scales, bits, master, moment, second)
 
 
-def reorder_kernel(mine_ref, others_ref, my_slots_ref, other_slots_ref, out_ref):
+def reorder_kernel(mine_ref, others_ref, my_slots_ref, other_slots_ref, out_ref, order_ref):
     blocks = out_ref.shape[0]
     half = mine_ref.shape[0]
-    row = lax.broadcasted_iota(jnp.int32, (blocks, half), 0)
-    my_order = (row == my_slots_ref[...]).astype(jnp.float32).astype(jnp.bfloat16)
-    other_order = (row == other_slots_ref[...]).astype(jnp.float32).astype(jnp.bfloat16)
-    order = jnp.concatenate([my_order, other_order], axis=1)
+
+    @pl.when(pl.program_id(0) == 0)
+    def _():
+        row = lax.broadcasted_iota(jnp.int32, (blocks, half), 0)
+        my_order = (row == my_slots_ref[...]).astype(jnp.float32).astype(jnp.bfloat16)
+        other_order = (row == other_slots_ref[...]).astype(jnp.float32).astype(jnp.bfloat16)
+        order_ref[...] = jnp.concatenate([my_order, other_order], axis=1)
+
     here = pl.ds(pl.multiple_of(pl.program_id(0) * out_ref.shape[1], LANES), out_ref.shape[1])
     held = jnp.concatenate([mine_ref[:, here], others_ref[:, here]], axis=0)
-    out_ref[...] = jnp.dot(order, held, preferred_element_type=jnp.float32).astype(jnp.bfloat16)
+    out_ref[...] = jnp.dot(order_ref[...], held, preferred_element_type=jnp.float32).astype(jnp.bfloat16)
 
 
 def reorder(mine, others, my_slots, other_slots):
     half, block = mine.shape
-    columns = 1024
+    columns = 2048
     return pl.pallas_call(
         reorder_kernel,
         grid=(block // columns,),
@@ -424,6 +428,7 @@
         ],
         out_specs=pl.BlockSpec((2 * half, columns), lambda i: (0, i)),
         out_shape=jax.ShapeDtypeStruct((2 * half, block), jnp.bfloat16),
+        scratch_shapes=[pltpu.VMEM((2 * half, 2 * half), jnp.bfloat16)],
         compiler_params=pltpu.CompilerParams(vmem_limit_bytes=VMEM_BYTES),
         name="reorder",
     )(mine, others, my_slots, other_slots)

time: 86.2 us -> 84.3 us (0.978)
  Pallas kernels: 22.5 us -> 21.2 us
where the time goes in v6:
time: 84.3 us; the launch traced here: 84 us
  blocking collectives  33.2 us (39%)
  Pallas kernels  21.2 us (25%)
  waiting for transfers between devices  19.4 us (23%)
  starting transfers between devices  7.81 us (9%)
  other arithmetic  1.24 us (1%)
    all_to_all x1, blocking collectives, local(): mine = lax.all_to_all(copies, chips, 0, 0, tiled=True)  17.5 us
    all_to_all x1, waiting for transfers between devices, local(): pairs = lax.all_to_all(pairs, chips, 0, 0, tiled=True)  17.5 us
    all_to_all x1, blocking collectives, local(): peaks = lax.all_to_all(peaks, axes, 0, 0, tiled=True)  15.7 us
    pallas_call x1, Pallas kernels, encode(): pl.pallas_call(functools.partial(encode_kernel, core), grid=(block // col...  7.51 us
    pallas_call x2, Pallas kernels, decode(): pl.pallas_call(decode_kernel, in_specs=[pl.BlockSpec(memory_space=pltpu.S...  5.53 us
    pallas_call x1, Pallas kernels, rotate(): pl.pallas_call(rotate_kernel, grid=(blocks // rows,), in_specs=[pl.BlockS...  4.96 us
    all_to_all x1, starting transfers between devices, local(): pairs = lax.all_to_all(pairs, chips, 0, 0, tiled=True)  3.8 us
    ppermute x1, starting transfers between devices, local(): others = lax.ppermute(mine, core, OTHER_CORE)  3.54 us
  transfers between devices with their start and end apart: 3, of which 2 were waited for; matrix products, arithmetic and copies ran while one was open for 0% of the time, Pallas kernels for 3%

profile of v6, /device:TPU:1, one launch (start us, length us, event | category | flops | bytes accessed | tf_op | source)
XLA Modules:
  0.0 84.0 jit_solution(8546868418446921755)
XLA Ops:
  0.6 0.0 copy-start
  0.6 0.0 copy-start.5
  0.7 0.0 copy-start.6
  0.7 5.0 %rotate.1 = (f32[256,4096]{1,0:T(8,128)S(1)}, f32[32,2,128]{2,1,0:T(2,128)S(1)}) custom-call(f32[256,4096]{1,0:T(8,128)} %bitcast.25, s32[1,4096]{1,0:T(1,128)} %bitcast.22), custom_call_target="tpu_custom_call" | custom-call | tf_op jit(solution)/shard_map/rotate/pallas_call | solution.py:106
  5.6 15.7 %all_to_all.15.peaks_ref = f32[32,2,128]{2,1,0:T(2,128)S(1)} all-to-all(f32[32,2,128]{2,1,0:T(2,128)S(1)} %get-tuple-element.20), channel_id=1, replica_groups=mesh['section'=4,'dp_chip'=16,'dp_core'=2] {'dp_chip','dp_core'}, dimensions={0} | all-to-all | bytes 65536 | tf_op jit(solution)/shard_map/all_to_all | solution.py:445
  21.3 0.0 copy-done
  21.3 0.0 copy-done.5
  21.3 0.0 copy-done.6
  21.3 7.5 %encode.1 = (bf16[128,4096]{1,0:T(8,128)(2,1)S(1)}, bf16[128,4096]{1,0:T(8,128)(2,1)S(1)}, f32[256,128]{1,0:T(8,128)S(1)}) custom-call(f32[16]{0:T(128)S(1)} %copy-done.5, f32[256,4096]{1,0:T(8,128)S(1)} %get-tuple-element.18.rotated_ref, s32[256,4096]{1,0:T(8,128)S(1)} %bitcast.17, f32[32,2,128]{2,1,0:T(2,128)S(1)} %all_to_all.15.peaks_ref, ...), custom_call_target="tpu_custom_call" | custom-call | tf_op jit(solution)/shard_map/encode/pallas_call | solution.py:243
  28.8 0.5 collective-permute-start
  29.3 2.8 %decode.2.refs_0_ = f32[128,4096]{1,0:T(8,128)S(1)} custom-call(f32[16]{0:T(128)S(1)} %copy-done.5, bf16[128,4096]{1,0:T(8,128)(2,1)S(1)} %get-tuple-element.22.symbols_ref), custom_call_target="tpu_custom_call" | custom-call | flops 25165824 | bytes 3145728 | tf_op jit(solution)/shard_map/decode/pallas_call | solution.py:337
  32.1 0.0 collective-permute-done.symbols_ref
  32.1 2.7 %decode.3 = f32[128,4096]{1,0:T(8,128)S(1)} custom-call(f32[16]{0:T(128)S(1)} %copy-done.5, bf16[128,4096]{1,0:T(8,128)(2,1)S(1)} %collective-permute-done.symbols_ref, f32[128,4096]{1,0:T(8,128)S(1)} %decode.2.refs_0_), custom_call_target="tpu_custom_call" | custom-call | flops 25165824 | bytes 3145728 | tf_op jit(solution)/shard_map/decode/pallas_call | solution.py:337
  34.8 1.1 %convert_bitcast_fusion = f16[16,8,4096]{2,1,0:T(8,128)(2,1)} fusion(f32[128,4096]{1,0:T(8,128)S(1)} %decode.3), kind=kLoop, calls=%fused_computation.1 | loop fusion | flops 524288 | bytes 3145728 | tf_op jit(solution)/shard_map/reshape | solution.py:449
  35.9 0.0 copy-start.1
  35.9 0.0 copy-start.2
  35.9 0.0 copy-start.3
  35.9 0.0 copy-start.4
  35.9 3.8 %all-to-all-start.1 = ((f16[16,8,4096]{2,1,0:T(8,128)(2,1)}), f16[16,8,4096]{2,1,0:T(8,128)(2,1)S(1)}, u32[]{:S(2)}, u32[]{:S(2)}) async-start(f16[16,8,4096]{2,1,0:T(8,128)(2,1)} %convert_bitcast_fusion), calls=%async_computation.1 | async-start | bytes 2097152 | tf_op jit(solution)/shard_map/all_to_all | solution.py:450
  39.7 17.5 %all-to-all-done.1 = f16[16,8,4096]{2,1,0:T(8,128)(2,1)S(1)} async-done(((f16[16,8,4096]{2,1,0:T(8,128)(2,1)}), f16[16,8,4096]{2,1,0:T(8,128)(2,1)S(1)}, u32[]{:S(2)}, u32[]{:S(2)}) %all-to-all-start.1) | async-done | bytes 1048608 | tf_op jit(solution)/shard_map/all_to_all | solution.py:450
  57.2 0.1 convert_reduce_fusion.total_ref
  57.4 0.0 copy-done.1
  57.4 0.0 copy-done.2
  57.4 0.0 copy-done.3
  57.4 0.0 copy-done.4
  57.4 1.3 %owner.1 = (f32[8,4096]{1,0:T(8,128)}, f32[8,4096]{1,0:T(8,128)}, f32[8,4096]{1,0:T(8,128)}, bf16[16,8,4096]{2,1,0:T(8,128)(2,1)S(1)}) custom-call(s32[1]{0:T(128)} %bitcast.place_ref, f32[8,4096]{1,0:T(8,128)S(1)} %convert_reduce_fusion.total_ref, f32[256,128]{1,0:T(8,128)S(1)} %get-tuple-element.23.scales_ref, s32[1,4096]{1,0:T(1,128)S(1)} %bitcast.23, ...), custom_call_target="tpu_custom_call" | custom-call | tf_op jit(solution)/shard_map/owner/pallas_call | solution.py:378
  58.7 17.5 %all_to_all.16 = bf16[16,8,4096]{2,1,0:T(8,128)(2,1)S(1)} all-to-all(bf16[16,8,4096]{2,1,0:T(8,128)(2,1)S(1)} %get-tuple-element.27), channel_id=1, replica_groups=mesh['section'=4,'dp_chip'=16,'dp_core'=2] {'dp_chip'}, dimensions={0} | all-to-all | bytes 2097152 | tf_op jit(solution)/shard_map/all_to_all | solution.py:456
  76.3 3.5 %collective-permute-start.1 = (bf16[16,8,4096]{2,1,0:T(8,128)(2,1)S(1)}, bf16[16,8,4096]{2,1,0:T(8,128)(2,1)S(1)}, u32[]{:S(2)}, u32[]{:S(2)}) collective-permute-start(bf16[16,8,4096]{2,1,0:T(8,128)(2,1)S(1)} %all_to_all.16), channel_id=1, source_target_pairs={{0,1},{1,0},{2,3},{3,2},{4,5},{5,4},{6,7},{7,6},{8,9},{9,8},{10,11... | collective-permute-start | bytes 3145736 | tf_op jit(solution)/shard_map/ppermute | solution.py:457
  79.8 0.1 reshape.43
  79.9 0.1 dynamic-slice_reduce_fusion
  80.0 0.1 reshape.44.my_slots_ref
  80.1 0.1 reshape.45.other_slots_ref
  80.1 1.9 %collective-permute-done.1 = bf16[16,8,4096]{2,1,0:T(8,128)(2,1)S(1)} collective-permute-done((bf16[16,8,4096]{2,1,0:T(8,128)(2,1)S(1)}, bf16[16,8,4096]{2,1,0:T(8,128)(2,1)S(1)}, u32[]{:S(2)}, u32[]{:S(2)}) %collective-permute-start.1) | collective-permute-done | bytes 1048608 | tf_op jit(solution)/shard_map/ppermute | solution.py:457
  82.1 1.9 %reorder.1 = bf16[256,4096]{1,0:T(8,128)(2,1)} custom-call(bf16[128,4096]{1,0:T(8,128)(2,1)S(1)} %bitcast.16, bf16[128,4096]{1,0:T(8,128)(2,1)S(1)} %bitcast.18, s32[1,128]{1,0:T(1,128)S(1)} %reshape.44.my_slots_ref, s32[1,128]{1,0:T(1,128)S(1)} %reshape.45.other_slots_ref), custom_call_target="tpu_custom_call" | custom-call | tf_op jit(solution)/shard_map/reorder/pallas_call | solution.py:420
Async XLA Ops:
  0.6 20.7 %copy-start = (s32[1,1,256,4096]{3,2,1,0:T(8,128)S(1)}, s32[1,1,256,4096]{3,2,1,0:T(8,128)}, u32[]{:S(2)}) copy-start(s32[1,1,256,4096]{3,2,1,0:T(8,128)} %param.9) | copy-start | bytes 12582916
  0.6 20.7 %copy-start.5 = (f32[16]{0:T(128)S(1)}, f32[16]{0:T(128)}, u32[]{:S(2)}) copy-start(f32[16]{0:T(128)} %levels_ref.5) | copy-start | bytes 196
  0.7 20.6 %copy-start.6 = (s32[256]{0:T(256)S(1)}, s32[256]{0:T(256)}, u32[]{:S(2)}) copy-start(s32[256]{0:T(256)} %param.12) | copy-start | bytes 3076
  28.8 3.3 %collective-permute-start = (bf16[128,4096]{1,0:T(8,128)(2,1)S(1)}, bf16[128,4096]{1,0:T(8,128)(2,1)S(1)}, u32[]{:S(2)}, u32[]{:S(2)}) collective-permute-start(bf16[128,4096]{1,0:T(8,128)(2,1)S(1)} %get-tuple-element.21), channel_id=1, source_target_pairs={{0,1},{1,0},{2,3},{3,2},{4,5},{5,4},{6,7},{7,6},{8,9},{9,8},{10,11... | collective-permute-start | bytes 3145736 | tf_op jit(solution)/shard_map/ppermute | solution.py:447
  35.9 21.4 %copy-start.1 = (f32[1,8,4096]{2,1,0:T(8,128)S(1)}, f32[1,8,4096]{2,1,0:T(8,128)}, u32[]{:S(2)}) copy-start(f32[1,8,4096]{2,1,0:T(8,128)} %param.13) | copy-start | bytes 393220
  35.9 21.5 %copy-start.2 = (f32[1,8,4096]{2,1,0:T(8,128)S(1)}, f32[1,8,4096]{2,1,0:T(8,128)}, u32[]{:S(2)}) copy-start(f32[1,8,4096]{2,1,0:T(8,128)} %param.14) | copy-start | bytes 393220
  35.9 21.5 %copy-start.3 = (f32[1,8,4096]{2,1,0:T(8,128)S(1)}, f32[1,8,4096]{2,1,0:T(8,128)}, u32[]{:S(2)}) copy-start(f32[1,8,4096]{2,1,0:T(8,128)} %param.15) | copy-start | bytes 393220
  35.9 21.5 %copy-start.4 = (s32[4096]{0:T(1024)S(1)}, s32[4096]{0:T(1024)}, u32[]{:S(2)}) copy-start(s32[4096]{0:T(1024)} %param.10) | copy-start | bytes 49156
  35.9 21.3 %all-to-all-start.1 = ((f16[16,8,4096]{2,1,0:T(8,128)(2,1)}), f16[16,8,4096]{2,1,0:T(8,128)(2,1)S(1)}, u32[]{:S(2)}, u32[]{:S(2)}) async-start(f16[16,8,4096]{2,1,0:T(8,128)(2,1)} %convert_bitcast_fusion), calls=%async_computation.1 | async-start | bytes 2097152 | tf_op jit(solution)/shard_map/all_to_all | solution.py:450
  76.3 5.8 %collective-permute-start.1 = (bf16[16,8,4096]{2,1,0:T(8,128)(2,1)S(1)}, bf16[16,8,4096]{2,1,0:T(8,128)(2,1)S(1)}, u32[]{:S(2)}, u32[]{:S(2)}) collective-permute-start(bf16[16,8,4096]{2,1,0:T(8,128)(2,1)S(1)} %all_to_all.16), channel_id=1, source_target_pairs={{0,1},{1,0},{2,3},{3,2},{4,5},{5,4},{6,7},{7,6},{8,9},{9,8},{10,11... | collective-permute-start | bytes 3145736 | tf_op jit(solution)/shard_map/ppermute | solution.py:457

commit v7 on v6

--- a/solution.py
+++ b/solution.py
@@ -189,7 +189,7 @@
             lines_ref[2 * number + 1] = intercept
 
     threshold, slope, intercept = tables_ref[0], tables_ref[1], tables_ref[2]
-    deep = 64
+    deep = 128
 
     def some_rows(number, carry):
         start = pl.multiple_of(number * deep, deep)
@@ -289,7 +289,7 @@
     out_ref = refs[-1]
     count = levels_ref.shape[0]
     rows, block = out_ref.shape
-    wide, deep = 1024, 64
+    wide, deep = 1024, 128
     slope, intercept = decode_tables(levels_ref)
     spacings = [levels_ref[level + 1] - levels_ref[level] for level in range(count - 1)]
     weights = [spacings[0]] + [spacings[level] - spacings[level - 1] for level in range(1, count - 1)] + [-spacings[-1]]

time: 84.3 us -> 83.7 us (level)
  no operation moved by 1% of the time
where the time goes in v7:
time: 83.7 us; the launch traced here: 83.5 us
  blocking collectives  33.1 us (40%)
  Pallas kernels  20.6 us (25%)
  waiting for transfers between devices  19.7 us (24%)
  starting transfers between devices  7.73 us (9%)
  other arithmetic  1.24 us (1%)
    all_to_all x1, waiting for transfers between devices, local(): pairs = lax.all_to_all(pairs, chips, 0, 0, tiled=True)  17.7 us
    all_to_all x1, blocking collectives, local(): mine = lax.all_to_all(copies, chips, 0, 0, tiled=True)  17.5 us
    all_to_all x1, blocking collectives, local(): peaks = lax.all_to_all(peaks, axes, 0, 0, tiled=True)  15.7 us
    pallas_call x1, Pallas kernels, encode(): pl.pallas_call(functools.partial(encode_kernel, core), grid=(block // col...  7.18 us
    pallas_call x2, Pallas kernels, decode(): pl.pallas_call(decode_kernel, in_specs=[pl.BlockSpec(memory_space=pltpu.S...  5.24 us
    pallas_call x1, Pallas kernels, rotate(): pl.pallas_call(rotate_kernel, grid=(blocks // rows,), in_specs=[pl.BlockS...  4.96 us
    all_to_all x1, starting transfers between devices, local(): pairs = lax.all_to_all(pairs, chips, 0, 0, tiled=True)  3.8 us
    ppermute x1, starting transfers between devices, local(): others = lax.ppermute(mine, core, OTHER_CORE)  3.46 us
  transfers between devices with their start and end apart: 3, of which 2 were waited for; matrix products, arithmetic and copies ran while one was open for 0% of the time, Pallas kernels for 3%

profile of v7, /device:TPU:1, one launch (start us, length us, event | category | flops | bytes accessed | tf_op | source)
XLA Modules:
  0.0 83.5 jit_solution(14600015468704260224)
XLA Ops:
  0.6 0.0 copy-start
  0.6 0.0 copy-start.5
  0.7 0.0 copy-start.6
  0.7 5.0 %rotate.1 = (f32[256,4096]{1,0:T(8,128)S(1)}, f32[32,2,128]{2,1,0:T(2,128)S(1)}) custom-call(f32[256,4096]{1,0:T(8,128)} %bitcast.25, s32[1,4096]{1,0:T(1,128)} %bitcast.22), custom_call_target="tpu_custom_call" | custom-call | tf_op jit(solution)/shard_map/rotate/pallas_call | solution.py:106
  5.6 15.7 %all_to_all.15.peaks_ref = f32[32,2,128]{2,1,0:T(2,128)S(1)} all-to-all(f32[32,2,128]{2,1,0:T(2,128)S(1)} %get-tuple-element.20), channel_id=1, replica_groups=mesh['section'=4,'dp_chip'=16,'dp_core'=2] {'dp_chip','dp_core'}, dimensions={0} | all-to-all | bytes 65536 | tf_op jit(solution)/shard_map/all_to_all | solution.py:445
  21.3 0.0 copy-done
  21.3 0.0 copy-done.5
  21.3 0.0 copy-done.6
  21.3 7.2 %encode.1 = (bf16[128,4096]{1,0:T(8,128)(2,1)S(1)}, bf16[128,4096]{1,0:T(8,128)(2,1)S(1)}, f32[256,128]{1,0:T(8,128)S(1)}) custom-call(f32[16]{0:T(128)S(1)} %copy-done.5, f32[256,4096]{1,0:T(8,128)S(1)} %get-tuple-element.18.rotated_ref, s32[256,4096]{1,0:T(8,128)S(1)} %bitcast.17, f32[32,2,128]{2,1,0:T(2,128)S(1)} %all_to_all.15.peaks_ref, ...), custom_call_target="tpu_custom_call" | custom-call | tf_op jit(solution)/shard_map/encode/pallas_call | solution.py:243
  28.5 0.5 collective-permute-start
  29.0 2.6 %decode.2.refs_0_ = f32[128,4096]{1,0:T(8,128)S(1)} custom-call(f32[16]{0:T(128)S(1)} %copy-done.5, bf16[128,4096]{1,0:T(8,128)(2,1)S(1)} %get-tuple-element.22.symbols_ref), custom_call_target="tpu_custom_call" | custom-call | flops 25165824 | bytes 3145728 | tf_op jit(solution)/shard_map/decode/pallas_call | solution.py:337
  31.6 0.0 collective-permute-done.symbols_ref
  31.6 2.6 %decode.3 = f32[128,4096]{1,0:T(8,128)S(1)} custom-call(f32[16]{0:T(128)S(1)} %copy-done.5, bf16[128,4096]{1,0:T(8,128)(2,1)S(1)} %collective-permute-done.symbols_ref, f32[128,4096]{1,0:T(8,128)S(1)} %decode.2.refs_0_), custom_call_target="tpu_custom_call" | custom-call | flops 25165824 | bytes 3145728 | tf_op jit(solution)/shard_map/decode/pallas_call | solution.py:337
  34.2 1.1 %convert_bitcast_fusion = f16[16,8,4096]{2,1,0:T(8,128)(2,1)} fusion(f32[128,4096]{1,0:T(8,128)S(1)} %decode.3), kind=kLoop, calls=%fused_computation.1 | loop fusion | flops 524288 | bytes 3145728 | tf_op jit(solution)/shard_map/reshape | solution.py:449
  35.3 0.0 copy-start.1
  35.3 0.0 copy-start.2
  35.3 0.0 copy-start.3
  35.3 0.0 copy-start.4
  35.3 3.8 %all-to-all-start.1 = ((f16[16,8,4096]{2,1,0:T(8,128)(2,1)}), f16[16,8,4096]{2,1,0:T(8,128)(2,1)S(1)}, u32[]{:S(2)}, u32[]{:S(2)}) async-start(f16[16,8,4096]{2,1,0:T(8,128)(2,1)} %convert_bitcast_fusion), calls=%async_computation.1 | async-start | bytes 2097152 | tf_op jit(solution)/shard_map/all_to_all | solution.py:450
  39.1 17.7 %all-to-all-done.1 = f16[16,8,4096]{2,1,0:T(8,128)(2,1)S(1)} async-done(((f16[16,8,4096]{2,1,0:T(8,128)(2,1)}), f16[16,8,4096]{2,1,0:T(8,128)(2,1)S(1)}, u32[]{:S(2)}, u32[]{:S(2)}) %all-to-all-start.1) | async-done | bytes 1048608 | tf_op jit(solution)/shard_map/all_to_all | solution.py:450
  56.8 0.1 convert_reduce_fusion.total_ref
  57.0 0.0 copy-done.1
  57.0 0.0 copy-done.2
  57.0 0.0 copy-done.3
  57.0 0.0 copy-done.4
  57.0 1.3 %owner.1 = (f32[8,4096]{1,0:T(8,128)}, f32[8,4096]{1,0:T(8,128)}, f32[8,4096]{1,0:T(8,128)}, bf16[16,8,4096]{2,1,0:T(8,128)(2,1)S(1)}) custom-call(s32[1]{0:T(128)} %bitcast.place_ref, f32[8,4096]{1,0:T(8,128)S(1)} %convert_reduce_fusion.total_ref, f32[256,128]{1,0:T(8,128)S(1)} %get-tuple-element.23.scales_ref, s32[1,4096]{1,0:T(1,128)S(1)} %bitcast.23, ...), custom_call_target="tpu_custom_call" | custom-call | tf_op jit(solution)/shard_map/owner/pallas_call | solution.py:378
  58.4 17.5 %all_to_all.16 = bf16[16,8,4096]{2,1,0:T(8,128)(2,1)S(1)} all-to-all(bf16[16,8,4096]{2,1,0:T(8,128)(2,1)S(1)} %get-tuple-element.27), channel_id=1, replica_groups=mesh['section'=4,'dp_chip'=16,'dp_core'=2] {'dp_chip'}, dimensions={0} | all-to-all | bytes 2097152 | tf_op jit(solution)/shard_map/all_to_all | solution.py:456
  75.8 3.5 %collective-permute-start.1 = (bf16[16,8,4096]{2,1,0:T(8,128)(2,1)S(1)}, bf16[16,8,4096]{2,1,0:T(8,128)(2,1)S(1)}, u32[]{:S(2)}, u32[]{:S(2)}) collective-permute-start(bf16[16,8,4096]{2,1,0:T(8,128)(2,1)S(1)} %all_to_all.16), channel_id=1, source_target_pairs={{0,1},{1,0},{2,3},{3,2},{4,5},{5,4},{6,7},{7,6},{8,9},{9,8},{10,11... | collective-permute-start | bytes 3145736 | tf_op jit(solution)/shard_map/ppermute | solution.py:457
  79.3 0.1 reshape.43
  79.4 0.1 dynamic-slice_reduce_fusion
  79.5 0.1 reshape.44.my_slots_ref
  79.5 0.1 reshape.45.other_slots_ref
  79.6 1.9 %collective-permute-done.1 = bf16[16,8,4096]{2,1,0:T(8,128)(2,1)S(1)} collective-permute-done((bf16[16,8,4096]{2,1,0:T(8,128)(2,1)S(1)}, bf16[16,8,4096]{2,1,0:T(8,128)(2,1)S(1)}, u32[]{:S(2)}, u32[]{:S(2)}) %collective-permute-start.1) | collective-permute-done | bytes 1048608 | tf_op jit(solution)/shard_map/ppermute | solution.py:457
  81.6 1.9 %reorder.1 = bf16[256,4096]{1,0:T(8,128)(2,1)} custom-call(bf16[128,4096]{1,0:T(8,128)(2,1)S(1)} %bitcast.16, bf16[128,4096]{1,0:T(8,128)(2,1)S(1)} %bitcast.18, s32[1,128]{1,0:T(1,128)S(1)} %reshape.44.my_slots_ref, s32[1,128]{1,0:T(1,128)S(1)} %reshape.45.other_slots_ref), custom_call_target="tpu_custom_call" | custom-call | tf_op jit(solution)/shard_map/reorder/pallas_call | solution.py:420
Async XLA Ops:
  0.6 20.7 %copy-start = (s32[1,1,256,4096]{3,2,1,0:T(8,128)S(1)}, s32[1,1,256,4096]{3,2,1,0:T(8,128)}, u32[]{:S(2)}) copy-start(s32[1,1,256,4096]{3,2,1,0:T(8,128)} %param.9) | copy-start | bytes 12582916
  0.6 20.7 %copy-start.5 = (f32[16]{0:T(128)S(1)}, f32[16]{0:T(128)}, u32[]{:S(2)}) copy-start(f32[16]{0:T(128)} %levels_ref.5) | copy-start | bytes 196
  0.7 20.6 %copy-start.6 = (s32[256]{0:T(256)S(1)}, s32[256]{0:T(256)}, u32[]{:S(2)}) copy-start(s32[256]{0:T(256)} %param.12) | copy-start | bytes 3076
  28.5 3.1 %collective-permute-start = (bf16[128,4096]{1,0:T(8,128)(2,1)S(1)}, bf16[128,4096]{1,0:T(8,128)(2,1)S(1)}, u32[]{:S(2)}, u32[]{:S(2)}) collective-permute-start(bf16[128,4096]{1,0:T(8,128)(2,1)S(1)} %get-tuple-element.21), channel_id=1, source_target_pairs={{0,1},{1,0},{2,3},{3,2},{4,5},{5,4},{6,7},{7,6},{8,9},{9,8},{10,11... | collective-permute-start | bytes 3145736 | tf_op jit(solution)/shard_map/ppermute | solution.py:447
  35.3 21.7 %copy-start.1 = (f32[1,8,4096]{2,1,0:T(8,128)S(1)}, f32[1,8,4096]{2,1,0:T(8,128)}, u32[]{:S(2)}) copy-start(f32[1,8,4096]{2,1,0:T(8,128)} %param.13) | copy-start | bytes 393220
  35.3 21.7 %copy-start.2 = (f32[1,8,4096]{2,1,0:T(8,128)S(1)}, f32[1,8,4096]{2,1,0:T(8,128)}, u32[]{:S(2)}) copy-start(f32[1,8,4096]{2,1,0:T(8,128)} %param.14) | copy-start | bytes 393220
  35.3 21.7 %copy-start.3 = (f32[1,8,4096]{2,1,0:T(8,128)S(1)}, f32[1,8,4096]{2,1,0:T(8,128)}, u32[]{:S(2)}) copy-start(f32[1,8,4096]{2,1,0:T(8,128)} %param.15) | copy-start | bytes 393220
  35.3 21.7 %copy-start.4 = (s32[4096]{0:T(1024)S(1)}, s32[4096]{0:T(1024)}, u32[]{:S(2)}) copy-start(s32[4096]{0:T(1024)} %param.10) | copy-start | bytes 49156
  35.3 21.5 %all-to-all-start.1 = ((f16[16,8,4096]{2,1,0:T(8,128)(2,1)}), f16[16,8,4096]{2,1,0:T(8,128)(2,1)S(1)}, u32[]{:S(2)}, u32[]{:S(2)}) async-start(f16[16,8,4096]{2,1,0:T(8,128)(2,1)} %convert_bitcast_fusion), calls=%async_computation.1 | async-start | bytes 2097152 | tf_op jit(solution)/shard_map/all_to_all | solution.py:450
  75.8 5.7 %collective-permute-start.1 = (bf16[16,8,4096]{2,1,0:T(8,128)(2,1)S(1)}, bf16[16,8,4096]{2,1,0:T(8,128)(2,1)S(1)}, u32[]{:S(2)}, u32[]{:S(2)}) collective-permute-start(bf16[16,8,4096]{2,1,0:T(8,128)(2,1)S(1)} %all_to_all.16), channel_id=1, source_target_pairs={{0,1},{1,0},{2,3},{3,2},{4,5},{5,4},{6,7},{7,6},{8,9},{9,8},{10,11... | collective-permute-start | bytes 3145736 | tf_op jit(solution)/shard_map/ppermute | solution.py:457
